TPU v7x, 1024 devices: a whole 4x8x16 slice. The times are simulated.
1024 devices in a mesh: seq: 64 (over x, z), tp: 16 (over y, core).
Axes of the slice: x: 4, y: 8, z: 16, core: 2. Of those that a mesh axis runs over, the one named last changes fastest.
Arguments:
- queries: bfloat16 [16384, 8192], P('seq', 'tp'), may hold values from -6 to 6
- keys: bfloat16 [16384, 8192], P('seq', 'tp'), may hold values from -6 to 6
- values: bfloat16 [16384, 8192], P('seq', 'tp'), may hold values from -6 to 6
- norm_gain: float32 [128], replicated, may hold values from 0.1 to 1.9
- out_weight: bfloat16 [8192, 8192], P(None, 'tp'), may hold values from -0.0625 to 0.0625
Outputs:
- layer_out: bfloat16 [16384, 8192], P('seq', 'tp')
All inputs are finite; a program needn't handle non-finite values.
Results may differ from a plain program's by a relative error of at most 0.0058.
Values may be sent and summed in bfloat16 or wider, within the bound.
No kernel may reach another device: no remote copies, remote signals or barrier semaphores. Data moves between devices by JAX's collectives and lax.ppermute only.
A program may use at most 32 MiB of HBM per device.

v0:
```python
import functools

import jax
import jax.numpy as jnp
from jax import lax
from jax.experimental import pallas as pl
from jax.experimental.pallas import tpu as pltpu
from jax.sharding import PartitionSpec as P

DH = 128

epsilon = 1e-06


VMEM = pl.BlockSpec(memory_space=pltpu.VMEM)
SMEM = pl.BlockSpec(memory_space=pltpu.SMEM)
PARAMS = pltpu.CompilerParams(vmem_limit_bytes=12 * 2**20)
WIDE = pltpu.CompilerParams(vmem_limit_bytes=50 * 2**20)
HBM = pl.BlockSpec(memory_space=pltpu.HBM)


def local_kernel(q_ref, k_ref, v_ref, g_ref, s_ref, w_ref, qo_ref, go_ref):
    rows = q_ref.shape[0]
    heads = [slice(h, h + DH) for h in range(0, q_ref.shape[1], DH)]
    for cols in heads:
        s_ref[cols, :] = lax.dot_general(
            k_ref[:, cols],
            v_ref[:, cols],
            (((0,), (0,)), ((), ())),
            preferred_element_type=jnp.float32,
        ).astype(s_ref.dtype)
    row_ids = lax.broadcasted_iota(jnp.int32, (rows, rows), 0)
    col_ids = lax.broadcasted_iota(jnp.int32, (rows, rows), 1)
    causal = col_ids <= row_ids
    for cols in heads:
        scores = lax.dot_general(
            q_ref[:, cols],
            k_ref[:, cols],
            (((1,), (1,)), ((), ())),
            preferred_element_type=jnp.float32,
        )
        scores = jnp.where(causal, scores, 0.0).astype(jnp.bfloat16)
        w_ref[:, cols] = jnp.dot(scores, v_ref[:, cols], preferred_element_type=jnp.float32)
    qo_ref[...] = q_ref[...]
    go_ref[...] = g_ref[...]


def scan_kernel(a_ref, p_ref):
    total = jnp.zeros(a_ref.shape[1:], jnp.float32)
    for c in range(a_ref.shape[0]):
        p_ref[c] = total.astype(p_ref.dtype)
        total = total + a_ref[c].astype(jnp.float32)


def attend_kernel(q_ref, w_ref, p_ref, g_ref, o_ref):
    for h in range(0, q_ref.shape[1], DH):
        cols = slice(h, h + DH)
        attended = jnp.dot(q_ref[:, cols], p_ref[cols, :], preferred_element_type=jnp.float32)
        attended = attended + w_ref[:, cols]
        mean = jnp.mean(attended * attended, axis=-1, keepdims=True)
        o_ref[:, cols] = (attended * lax.rsqrt(mean + epsilon) * g_ref[...]).astype(o_ref.dtype)


def source(me, ring, step, other):
    core = lax.rem(me, 2)
    at = lax.div(me, 2) + jnp.where(core == 0, ring - step, step)
    return 2 * lax.rem(at, ring) + (1 - core if other else core)


def project_kernel(ring, step, other, weights, seeded, me_ref, block_ref, *refs):
    count = len(weights)
    weight_refs, refs = refs[:2], refs[2:]
    seeds = refs[:count] if seeded else None
    outs = refs[count if seeded else 0 :][:count]
    slots, sems = refs[-2:]
    depth = slots.shape[1]
    at = pl.multiple_of(source(me_ref[0], ring, step, other) * depth, depth)
    copies = []
    for n, w in enumerate(weights):
        rows = weight_refs[w].at[pl.ds(at, depth), :]
        copies.append(pltpu.make_async_copy(rows, slots.at[n], sems.at[n]))
        copies[-1].start()
    for n in range(count):
        copies[n].wait()
        part = jnp.dot(block_ref[...], slots[n], preferred_element_type=jnp.float32)
        outs[n][...] = seeds[n][...] + part if seeded else part


def project(me, ring, step, other, block, columns, weights, seeds=()):
    rows, depth = block.shape
    cols = columns[0].shape[1]
    count = len(weights)
    return pl.pallas_call(
        functools.partial(project_kernel, ring, step, other, weights, bool(seeds)),
        out_shape=[jax.ShapeDtypeStruct((rows, cols), jnp.float32)] * count,
        in_specs=[SMEM, VMEM, HBM, HBM] + [VMEM] * len(seeds),
        out_specs=[VMEM] * count,
        scratch_shapes=[
            pltpu.VMEM((count, depth, cols), columns[0].dtype),
            pltpu.SemaphoreType.DMA((count,)),
        ],
        compiler_params=WIDE,
        cost_estimate=pl.CostEstimate(
            flops=2 * rows * depth * cols * count,
            bytes_accessed=count * depth * cols * 2,
            transcendentals=0,
        ),
    )(me.reshape(1), block, *columns, *seeds)


def pair_kernel(ring, step, me_ref, pair_ref, w_ref, seed_ref, *refs):
    more, (out_ref, slots, sems) = refs[:-3], refs[-3:]
    rows = seed_ref.shape[0]
    depth = slots.shape[1]
    chip = source(me_ref[0], ring, step, False) // 2
    copies = []
    for n in range(2):
        at = pl.multiple_of((2 * chip + n) * depth, depth)
        copies.append(pltpu.make_async_copy(w_ref.at[pl.ds(at, depth), :], slots.at[n], sems.at[n]))
        copies[-1].start()
    total = seed_ref[...]
    for ref in more:
        total = total + ref[...]
    for n in range(2):
        copies[n].wait()
        block = pair_ref[n * rows : (n + 1) * rows, :]
        total = total + jnp.dot(block, slots[n], preferred_element_type=jnp.float32)
    out_ref[...] = total.astype(out_ref.dtype)


def project_pair(me, ring, step, pair, weight, dtype, *seeds):
    rows, cols = seeds[0].shape
    depth = pair.shape[1]
    return pl.pallas_call(
        functools.partial(pair_kernel, ring, step),
        out_shape=jax.ShapeDtypeStruct((rows, cols), dtype),
        in_specs=[SMEM, VMEM, HBM] + [VMEM] * len(seeds),
        out_specs=VMEM,
        scratch_shapes=[
            pltpu.VMEM((2, depth, cols), weight.dtype),
            pltpu.SemaphoreType.DMA((2,)),
        ],
        compiler_params=WIDE,
        cost_estimate=pl.CostEstimate(
            flops=4 * rows * depth * cols,
            bytes_accessed=2 * depth * cols * 2,
            transcendentals=0,
        ),
    )(me.reshape(1), pair, weight, *seeds)


def call(kernel, shape, dtype, args, flops):
    size = sum(a.size * a.dtype.itemsize for a in args)
    return pl.pallas_call(
        kernel,
        out_shape=jax.ShapeDtypeStruct(shape, dtype),
        in_specs=[VMEM] * len(args),
        out_specs=VMEM,
        compiler_params=PARAMS,
        cost_estimate=pl.CostEstimate(flops=flops, bytes_accessed=size, transcendentals=0),
    )(*args)


def local(queries, keys, values, gain):
    rows, width = queries.shape
    return pl.pallas_call(
        local_kernel,
        out_shape=[
            jax.ShapeDtypeStruct((width, DH), jnp.bfloat16),
            jax.ShapeDtypeStruct((rows, width), jnp.float32),
            jax.ShapeDtypeStruct((rows, width), queries.dtype),
            jax.ShapeDtypeStruct(gain.shape, gain.dtype),
        ],
        in_specs=[VMEM] * 4,
        out_specs=[VMEM] * 4,
        compiler_params=PARAMS,
        cost_estimate=pl.CostEstimate(
            flops=2 * rows * width * (DH + 2 * rows),
            bytes_accessed=3 * rows * width * 2,
            transcendentals=0,
        ),
    )(queries, keys, values, gain)


def on_device(queries, keys, values, norm_gain, out_weight):
    rows, width = queries.shape
    groups = lax.axis_size("seq")
    tp = lax.axis_size("tp")
    ring = tp // 2
    me = lax.axis_index("tp")
    partner = [(j, j ^ 1) for j in range(tp)]
    onward = [
        (2 * y + c, 2 * ((y + (1, -1)[c]) % ring) + c) for y in range(ring) for c in range(2)
    ]
    across = [(s ^ 1, d) for s, d in onward]
    tie = lax.optimization_barrier

    states, within, near_queries, gain = local(
        queries, keys, values, norm_gain.reshape(1, DH)
    )
    weight, states = tie((out_weight, states))
    columns = (out_weight, lax.ppermute(weight, "tp", partner))
    slices = states.reshape(groups, width // groups, DH)
    slices = lax.all_to_all(slices, "seq", 0, 0, tiled=True)
    prefix = call(scan_kernel, slices.shape, jnp.bfloat16, (slices,), slices.size)
    prefix = lax.all_to_all(prefix, "seq", 0, 0, tiled=True).reshape(width, DH)
    own = call(
        attend_kernel,
        (rows, width),
        jnp.bfloat16,
        (near_queries, within, prefix, gain),
        2 * rows * width * DH,
    )

    halves = [[2 * y, 2 * y + 1] for y in range(ring)]
    half = (ring - 1) // 2

    def send(block, pairs):
        return lax.ppermute(block, "tp", pairs)

    def multiply(step, other, block, sums):
        return project(me, ring, step, other, block, columns, (0, 1), sums)

    first = send(own, onward)
    second = send(own, across)
    sums = multiply(0, False, own, ())
    for step in range(1, half + 1):
        first, sums = tie((first, sums))
        sums = multiply(step, False, first, sums)
        first = send(first, onward)
        second, sums = tie((second, sums))
        sums = multiply(step, True, second, sums)
        if step < half:
            second = send(second, onward)
    mine, theirs = sums
    returned = send(theirs, partner)
    first, returned = tie((first, returned))
    pair = lax.all_gather(first, "tp", axis=0, tiled=True, axis_index_groups=halves)
    return project_pair(me, ring, half + 1, pair, out_weight, jnp.bfloat16, mine, returned)


def solution(mesh):
    return jax.shard_map(
        on_device,
        mesh=mesh,
        in_specs=(P("seq", "tp"), P("seq", "tp"), P("seq", "tp"), P(), P(None, "tp")),
        out_specs=P("seq", "tp"),
        check_vma=False,
    )
```

profile of v0, /device:TPU:1, one launch (start us, length us, event | category | flops | bytes accessed | tf_op | source)
XLA Modules:
  0.0 120.2 jit_solution(7769270594970284340)
XLA Ops:
  0.0 0.0 copy-start
  0.0 0.9 copy-done
  1.0 0.0 copy-start.1
  1.0 0.9 copy-done.1
  1.9 0.0 copy-start.2
  1.9 0.9 copy-done.2
  2.9 0.0 copy-start.3
  2.9 0.7 copy-done.3
  3.5 0.6 shard_map.55
  4.2 16.0 %collective-permute-start.1 = (bf16[8192,512]{1,0:T(8,128)(2,1)}, bf16[8192,512]{1,0:T(8,128)(2,1)}, u32[]{:S(2)}, u32[]{:S(2)}) collective-permute-start(bf16[8192,512]{1,0:T(8,128)(2,1)} %w_ref.1), channel_id=1, source_target_pairs={{0,1},{1,0},{2,3},{3,2},{4,5},{5,4},{6,7},{7,6},{8,9},{9,8},{10,11... | collective-permute-start | bytes 25165832 | tf_op jit(solution)/shard_map/ppermute | solution.py:202
  20.2 24.0 %all_to_all.10.a_ref = bf16[64,8,128]{2,1,0:T(8,128)(2,1)S(1)} all-to-all(bf16[64,8,128]{2,1,0:T(8,128)(2,1)S(1)} %bitcast.5), channel_id=1, replica_groups=mesh['seq'=64,'tp'=16] {'seq'}, dimensions={0} | all-to-all | bytes 262144 | tf_op jit(solution)/shard_map/all_to_all | solution.py:204
  44.2 0.1 shard_map.56
  44.3 20.9 %all_to_all.11 = bf16[64,8,128]{2,1,0:T(8,128)(2,1)S(1)} all-to-all(bf16[64,8,128]{2,1,0:T(8,128)(2,1)S(1)} %shard_map.56), channel_id=1, replica_groups=mesh['seq'=64,'tp'=16] {'seq'}, dimensions={0} | all-to-all | bytes 262144 | tf_op jit(solution)/shard_map/all_to_all | solution.py:206
  65.2 0.4 shard_map.57.block_ref
  65.6 5.1 %collective-permute-start = (bf16[256,512]{1,0:T(8,128)(2,1)S(1)}, bf16[256,512]{1,0:T(8,128)(2,1)S(1)}, u32[]{:S(2)}, u32[]{:S(2)}) collective-permute-start(bf16[256,512]{1,0:T(8,128)(2,1)S(1)} %shard_map.57.block_ref), channel_id=1, source_target_pairs={{0,2},{1,15},{2,4},{3,1},{4,6},{5,3},{6,8},{7,5},{8,10},{9,7},{10,... | collective-permute-start | bytes 786440 | tf_op jit(solution)/shard_map/ppermute | solution.py:219
  70.7 4.6 %collective-permute-start.3 = (bf16[256,512]{1,0:T(8,128)(2,1)S(1)}, bf16[256,512]{1,0:T(8,128)(2,1)S(1)}, u32[]{:S(2)}, u32[]{:S(2)}) collective-permute-start(bf16[256,512]{1,0:T(8,128)(2,1)S(1)} %shard_map.57.block_ref), channel_id=1, source_target_pairs={{1,2},{0,15},{3,4},{2,1},{5,6},{4,3},{7,8},{6,5},{9,10},{8,7},{11,... | collective-permute-start | bytes 786440 | tf_op jit(solution)/shard_map/ppermute | solution.py:219
  75.3 0.0 collective-permute-done.1.refs_1_
  75.3 1.7 %shard_map.58 = (f32[256,512]{1,0:T(8,128)S(1)}, f32[256,512]{1,0:T(8,128)S(1)}) custom-call(s32[1]{0:T(128)} %bitcast.me_ref, bf16[256,512]{1,0:T(8,128)(2,1)S(1)} %shard_map.57.block_ref, bf16[8192,512]{1,0:T(8,128)(2,1)} %w_ref.1, bf16[8192,512]{1,0:T(8,128)(2,1)} %collective-permute-done.1.refs_1_), custom_call_target="tpu_custom_call" | custom-call | flops 268435456 | bytes 1048576 | tf_op jit(solution)/shard_map/pallas_call | solution.py:93
  77.0 0.0 collective-permute-done.block_ref
  77.0 3.3 %collective-permute-start.2 = (bf16[256,512]{1,0:T(8,128)(2,1)S(1)}, bf16[256,512]{1,0:T(8,128)(2,1)S(1)}, u32[]{:S(2)}, u32[]{:S(2)}) collective-permute-start(bf16[256,512]{1,0:T(8,128)(2,1)S(1)} %collective-permute-done.block_ref), channel_id=1, source_target_pairs={{0,2},{1,15},{2,4},{3,1},{4,6},{5,3},{6,8},{7,5},{8,10},{9,7},{10,... | collective-permute-start | bytes 786440 | tf_op jit(solution)/shard_map/ppermute | solution.py:219
  80.3 1.7 %shard_map.59 = (f32[256,512]{1,0:T(8,128)S(1)}, f32[256,512]{1,0:T(8,128)S(1)}) custom-call(s32[1]{0:T(128)} %bitcast.me_ref, bf16[256,512]{1,0:T(8,128)(2,1)S(1)} %collective-permute-done.block_ref, bf16[8192,512]{1,0:T(8,128)(2,1)} %w_ref.1, bf16[8192,512]{1,0:T(8,128)(2,1)} %collective-permute-done.1.refs_1_, f32[256,512]{1,0:T(8,128)S(1)} %get-tuple-element.54.refs_2_, ...), custom_call_target="tpu_custom_call" | custom-call | flops 268435456 | bytes 1048576 | tf_op jit(solution)/shard_map/pallas_call | solution.py:93
  81.9 0.0 collective-permute-done.3.block_ref
  82.0 2.3 %collective-permute-start.5 = (bf16[256,512]{1,0:T(8,128)(2,1)S(1)}, bf16[256,512]{1,0:T(8,128)(2,1)S(1)}, u32[]{:S(2)}, u32[]{:S(2)}) collective-permute-start(bf16[256,512]{1,0:T(8,128)(2,1)S(1)} %collective-permute-done.3.block_ref), channel_id=1, source_target_pairs={{0,2},{1,15},{2,4},{3,1},{4,6},{5,3},{6,8},{7,5},{8,10},{9,7},{10,... | collective-permute-start | bytes 786440 | tf_op jit(solution)/shard_map/ppermute | solution.py:219
  84.3 1.7 %shard_map.60 = (f32[256,512]{1,0:T(8,128)S(1)}, f32[256,512]{1,0:T(8,128)S(1)}) custom-call(s32[1]{0:T(128)} %bitcast.me_ref, bf16[256,512]{1,0:T(8,128)(2,1)S(1)} %collective-permute-done.3.block_ref, bf16[8192,512]{1,0:T(8,128)(2,1)} %w_ref.1, bf16[8192,512]{1,0:T(8,128)(2,1)} %collective-permute-done.1.refs_1_, ...), custom_call_target="tpu_custom_call" | custom-call | flops 268435456 | bytes 1048576 | tf_op jit(solution)/shard_map/pallas_call | solution.py:93
  86.0 0.0 collective-permute-done.2.block_ref
  86.0 3.6 %collective-permute-start.4 = (bf16[256,512]{1,0:T(8,128)(2,1)S(1)}, bf16[256,512]{1,0:T(8,128)(2,1)S(1)}, u32[]{:S(2)}, u32[]{:S(2)}) collective-permute-start(bf16[256,512]{1,0:T(8,128)(2,1)S(1)} %collective-permute-done.2.block_ref), channel_id=1, source_target_pairs={{0,2},{1,15},{2,4},{3,1},{4,6},{5,3},{6,8},{7,5},{8,10},{9,7},{10,... | collective-permute-start | bytes 786440 | tf_op jit(solution)/shard_map/ppermute | solution.py:219
  89.6 1.7 %shard_map.61 = (f32[256,512]{1,0:T(8,128)S(1)}, f32[256,512]{1,0:T(8,128)S(1)}) custom-call(s32[1]{0:T(128)} %bitcast.me_ref, bf16[256,512]{1,0:T(8,128)(2,1)S(1)} %collective-permute-done.2.block_ref, bf16[8192,512]{1,0:T(8,128)(2,1)} %w_ref.1, bf16[8192,512]{1,0:T(8,128)(2,1)} %collective-permute-done.1.refs_1_, ...), custom_call_target="tpu_custom_call" | custom-call | flops 268435456 | bytes 1048576 | tf_op jit(solution)/shard_map/pallas_call | solution.py:93
  91.3 0.0 collective-permute-done.5.block_ref
  91.3 3.0 %collective-permute-start.7 = (bf16[256,512]{1,0:T(8,128)(2,1)S(1)}, bf16[256,512]{1,0:T(8,128)(2,1)S(1)}, u32[]{:S(2)}, u32[]{:S(2)}) collective-permute-start(bf16[256,512]{1,0:T(8,128)(2,1)S(1)} %collective-permute-done.5.block_ref), channel_id=1, source_target_pairs={{0,2},{1,15},{2,4},{3,1},{4,6},{5,3},{6,8},{7,5},{8,10},{9,7},{10,... | collective-permute-start | bytes 786440 | tf_op jit(solution)/shard_map/ppermute | solution.py:219
  94.3 1.7 %shard_map.62 = (f32[256,512]{1,0:T(8,128)S(1)}, f32[256,512]{1,0:T(8,128)S(1)}) custom-call(s32[1]{0:T(128)} %bitcast.me_ref, bf16[256,512]{1,0:T(8,128)(2,1)S(1)} %collective-permute-done.5.block_ref, bf16[8192,512]{1,0:T(8,128)(2,1)} %w_ref.1, bf16[8192,512]{1,0:T(8,128)(2,1)} %collective-permute-done.1.refs_1_, ...), custom_call_target="tpu_custom_call" | custom-call | flops 268435456 | bytes 1048576 | tf_op jit(solution)/shard_map/pallas_call | solution.py:93
  96.0 0.0 collective-permute-done.4.block_ref
  96.0 1.7 %shard_map.63 = (f32[256,512]{1,0:T(8,128)S(1)}, f32[256,512]{1,0:T(8,128)S(1)}) custom-call(s32[1]{0:T(128)} %bitcast.me_ref, bf16[256,512]{1,0:T(8,128)(2,1)S(1)} %collective-permute-done.4.block_ref, bf16[8192,512]{1,0:T(8,128)(2,1)} %w_ref.1, bf16[8192,512]{1,0:T(8,128)(2,1)} %collective-permute-done.1.refs_1_, ...), custom_call_target="tpu_custom_call" | custom-call | flops 268435456 | bytes 1048576 | tf_op jit(solution)/shard_map/pallas_call | solution.py:93
  97.7 0.7 collective-permute-done.7.block_ref
  98.5 1.7 %shard_map.64 = (f32[256,512]{1,0:T(8,128)S(1)}, f32[256,512]{1,0:T(8,128)S(1)}) custom-call(s32[1]{0:T(128)} %bitcast.me_ref, bf16[256,512]{1,0:T(8,128)(2,1)S(1)} %collective-permute-done.7.block_ref, bf16[8192,512]{1,0:T(8,128)(2,1)} %w_ref.1, bf16[8192,512]{1,0:T(8,128)(2,1)} %collective-permute-done.1.refs_1_, ...), custom_call_target="tpu_custom_call" | custom-call | flops 268435456 | bytes 1048576 | tf_op jit(solution)/shard_map/pallas_call | solution.py:93
  100.1 6.5 %collective-permute-start.8 = (f32[256,512]{1,0:T(8,128)S(1)}, f32[256,512]{1,0:T(8,128)S(1)}, u32[]{:S(2)}, u32[]{:S(2)}) collective-permute-start(f32[256,512]{1,0:T(8,128)S(1)} %get-tuple-element.81), channel_id=1, source_target_pairs={{0,1},{1,0},{2,3},{3,2},{4,5},{5,4},{6,7},{7,6},{8,9},{9,8},{10,11... | collective-permute-start | bytes 1572872 | tf_op jit(solution)/shard_map/ppermute | solution.py:219
  106.6 1.9 %collective-permute-start.6 = (bf16[256,512]{1,0:T(8,128)(2,1)S(1)}, bf16[256,512]{1,0:T(8,128)(2,1)S(1)}, u32[]{:S(2)}, u32[]{:S(2)}) collective-permute-start(bf16[256,512]{1,0:T(8,128)(2,1)S(1)} %collective-permute-done.4.block_ref), channel_id=1, source_target_pairs={{0,2},{1,15},{2,4},{3,1},{4,6},{5,3},{6,8},{7,5},{8,10},{9,7},{10,... | collective-permute-start | bytes 786440 | tf_op jit(solution)/shard_map/ppermute | solution.py:219
  108.6 6.2 %collective-permute-done.6 = bf16[256,512]{1,0:T(8,128)(2,1)S(1)} collective-permute-done((bf16[256,512]{1,0:T(8,128)(2,1)S(1)}, bf16[256,512]{1,0:T(8,128)(2,1)S(1)}, u32[]{:S(2)}, u32[]{:S(2)}) %collective-permute-start.6) | collective-permute-done | bytes 262176 | tf_op jit(solution)/shard_map/ppermute | solution.py:219
  114.8 0.0 collective-permute-done.8.refs_0_
  114.8 3.1 %all_gather.3.pair_ref = bf16[512,512]{1,0:T(8,128)(2,1)S(1)} all-gather(bf16[256,512]{1,0:T(8,128)(2,1)S(1)} %collective-permute-done.6), channel_id=1, replica_groups={{0,1},{2,3},{4,5},{6,7},{8,9},{10,11},{12,13},{14,15},{16,17},{18,19},{..., dimensions={0}, use_global_device_ids=true | all-gather | bytes 786432 | tf_op jit(solution)/shard_map/all_gather | solution.py:238
  117.9 2.3 %shard_map.65 = bf16[256,512]{1,0:T(8,128)(2,1)} custom-call(s32[1]{0:T(128)} %bitcast.me_ref, bf16[512,512]{1,0:T(8,128)(2,1)S(1)} %all_gather.3.pair_ref, bf16[8192,512]{1,0:T(8,128)(2,1)} %w_ref.1, f32[256,512]{1,0:T(8,128)S(1)} %get-tuple-element.83.seed_ref, f32[256,512]{1,0:T(8,128)S(1)} %collective-permute-done.8.refs_0_), custom_call_target="tpu_custom_call" | custom-call | flops 268435456 | bytes 1048576 | tf_op jit(solution)/shard_map/pallas_call | solution.py:134
Async XLA Ops:
  0.0 0.9 copy-start
  1.0 0.9 copy-start.1
  1.9 0.9 copy-start.2
  2.9 0.7 copy-start.3
  4.2 71.1 %collective-permute-start.1 = (bf16[8192,512]{1,0:T(8,128)(2,1)}, bf16[8192,512]{1,0:T(8,128)(2,1)}, u32[]{:S(2)}, u32[]{:S(2)}) collective-permute-start(bf16[8192,512]{1,0:T(8,128)(2,1)} %w_ref.1), channel_id=1, source_target_pairs={{0,1},{1,0},{2,3},{3,2},{4,5},{5,4},{6,7},{7,6},{8,9},{9,8},{10,11... | collective-permute-start | bytes 25165832 | tf_op jit(solution)/shard_map/ppermute | solution.py:202
  65.6 11.4 %collective-permute-start = (bf16[256,512]{1,0:T(8,128)(2,1)S(1)}, bf16[256,512]{1,0:T(8,128)(2,1)S(1)}, u32[]{:S(2)}, u32[]{:S(2)}) collective-permute-start(bf16[256,512]{1,0:T(8,128)(2,1)S(1)} %shard_map.57.block_ref), channel_id=1, source_target_pairs={{0,2},{1,15},{2,4},{3,1},{4,6},{5,3},{6,8},{7,5},{8,10},{9,7},{10,... | collective-permute-start | bytes 786440 | tf_op jit(solution)/shard_map/ppermute | solution.py:219
  70.7 11.3 %collective-permute-start.3 = (bf16[256,512]{1,0:T(8,128)(2,1)S(1)}, bf16[256,512]{1,0:T(8,128)(2,1)S(1)}, u32[]{:S(2)}, u32[]{:S(2)}) collective-permute-start(bf16[256,512]{1,0:T(8,128)(2,1)S(1)} %shard_map.57.block_ref), channel_id=1, source_target_pairs={{1,2},{0,15},{3,4},{2,1},{5,6},{4,3},{7,8},{6,5},{9,10},{8,7},{11,... | collective-permute-start | bytes 786440 | tf_op jit(solution)/shard_map/ppermute | solution.py:219
  77.0 9.0 %collective-permute-start.2 = (bf16[256,512]{1,0:T(8,128)(2,1)S(1)}, bf16[256,512]{1,0:T(8,128)(2,1)S(1)}, u32[]{:S(2)}, u32[]{:S(2)}) collective-permute-start(bf16[256,512]{1,0:T(8,128)(2,1)S(1)} %collective-permute-done.block_ref), channel_id=1, source_target_pairs={{0,2},{1,15},{2,4},{3,1},{4,6},{5,3},{6,8},{7,5},{8,10},{9,7},{10,... | collective-permute-start | bytes 786440 | tf_op jit(solution)/shard_map/ppermute | solution.py:219
  82.0 9.4 %collective-permute-start.5 = (bf16[256,512]{1,0:T(8,128)(2,1)S(1)}, bf16[256,512]{1,0:T(8,128)(2,1)S(1)}, u32[]{:S(2)}, u32[]{:S(2)}) collective-permute-start(bf16[256,512]{1,0:T(8,128)(2,1)S(1)} %collective-permute-done.3.block_ref), channel_id=1, source_target_pairs={{0,2},{1,15},{2,4},{3,1},{4,6},{5,3},{6,8},{7,5},{8,10},{9,7},{10,... | collective-permute-start | bytes 786440 | tf_op jit(solution)/shard_map/ppermute | solution.py:219
  86.0 10.0 %collective-permute-start.4 = (bf16[256,512]{1,0:T(8,128)(2,1)S(1)}, bf16[256,512]{1,0:T(8,128)(2,1)S(1)}, u32[]{:S(2)}, u32[]{:S(2)}) collective-permute-start(bf16[256,512]{1,0:T(8,128)(2,1)S(1)} %collective-permute-done.2.block_ref), channel_id=1, source_target_pairs={{0,2},{1,15},{2,4},{3,1},{4,6},{5,3},{6,8},{7,5},{8,10},{9,7},{10,... | collective-permute-start | bytes 786440 | tf_op jit(solution)/shard_map/ppermute | solution.py:219
  91.3 7.1 %collective-permute-start.7 = (bf16[256,512]{1,0:T(8,128)(2,1)S(1)}, bf16[256,512]{1,0:T(8,128)(2,1)S(1)}, u32[]{:S(2)}, u32[]{:S(2)}) collective-permute-start(bf16[256,512]{1,0:T(8,128)(2,1)S(1)} %collective-permute-done.5.block_ref), channel_id=1, source_target_pairs={{0,2},{1,15},{2,4},{3,1},{4,6},{5,3},{6,8},{7,5},{8,10},{9,7},{10,... | collective-permute-start | bytes 786440 | tf_op jit(solution)/shard_map/ppermute | solution.py:219
  100.1 14.7 %collective-permute-start.8 = (f32[256,512]{1,0:T(8,128)S(1)}, f32[256,512]{1,0:T(8,128)S(1)}, u32[]{:S(2)}, u32[]{:S(2)}) collective-permute-start(f32[256,512]{1,0:T(8,128)S(1)} %get-tuple-element.81), channel_id=1, source_target_pairs={{0,1},{1,0},{2,3},{3,2},{4,5},{5,4},{6,7},{7,6},{8,9},{9,8},{10,11... | collective-permute-start | bytes 1572872 | tf_op jit(solution)/shard_map/ppermute | solution.py:219
  106.6 8.2 %collective-permute-start.6 = (bf16[256,512]{1,0:T(8,128)(2,1)S(1)}, bf16[256,512]{1,0:T(8,128)(2,1)S(1)}, u32[]{:S(2)}, u32[]{:S(2)}) collective-permute-start(bf16[256,512]{1,0:T(8,128)(2,1)S(1)} %collective-permute-done.4.block_ref), channel_id=1, source_target_pairs={{0,2},{1,15},{2,4},{3,1},{4,6},{5,3},{6,8},{7,5},{8,10},{9,7},{10,... | collective-permute-start | bytes 786440 | tf_op jit(solution)/shard_map/ppermute | solution.py:219
where the time goes:
time: 121 us; the launch traced here: 120 us
  blocking collectives  48 us (40%)
  starting transfers between devices  46.4 us (38%)
  Pallas kernels  15.1 us (12%)
  waiting for transfers between devices  6.99 us (6%)
  local copies, waits for them, and re-layouts  3.5 us (3%)
    ppermute x8, starting transfers between devices, send(): return lax.ppermute(block, 'tp', pairs)  30.4 us
    all_to_all x1, blocking collectives, on_device(): slices = lax.all_to_all(slices, 'seq', 0, 0, tiled=True)  24 us
    all_to_all x1, blocking collectives, on_device(): prefix = lax.all_to_all(prefix, 'seq', 0, 0, tiled=True).reshape(width, DH)  20.9 us
    ppermute x1, starting transfers between devices, on_device(): columns = (out_weight, lax.ppermute(weight, 'tp', partner))  16 us
    pallas_call x7, Pallas kernels, project(): pl.pallas_call(functools.partial(project_kernel, ring, step, other, weigh...  11.7 us
    ppermute x8, waiting for transfers between devices, send(): return lax.ppermute(block, 'tp', pairs)  6.99 us
    unnamed x8, local copies, waits for them, and re-layouts  3.5 us
    all_gather x1, blocking collectives, on_device(): lax.all_gather(first, 'tp', axis=0, tiled=True, axis_index_groups=halves)  3.13 us
  transfers between devices with their start and end apart: 9, of which 2 were waited for; matrix products, arithmetic and copies ran while one was open for 0% of the time, Pallas kernels for 9%

commit v1 on v0

v1 whole, which is shorter than its diff:
```python
import functools

import jax
import jax.numpy as jnp
from jax import lax
from jax.experimental import pallas as pl
from jax.experimental.pallas import tpu as pltpu
from jax.sharding import PartitionSpec as P

DH = 128

epsilon = 1e-06


VMEM = pl.BlockSpec(memory_space=pltpu.VMEM)
SMEM = pl.BlockSpec(memory_space=pltpu.SMEM)
PARAMS = pltpu.CompilerParams(vmem_limit_bytes=12 * 2**20)
HBM = pl.BlockSpec(memory_space=pltpu.HBM)


def local_kernel(q_hbm, k_hbm, v_hbm, g_hbm, s_ref, w_ref, q_ref, g_ref, k_ref, v_ref, sems):
    pairs = ((k_hbm, k_ref), (v_hbm, v_ref), (q_hbm, q_ref), (g_hbm, g_ref))
    copies = [pltpu.make_async_copy(a, b, sems.at[n]) for n, (a, b) in enumerate(pairs)]
    for copy in copies:
        copy.start()
    rows = q_ref.shape[0]
    heads = [slice(h, h + DH) for h in range(0, q_ref.shape[1], DH)]
    copies[0].wait()
    copies[1].wait()
    for cols in heads:
        s_ref[cols, :] = lax.dot_general(
            k_ref[:, cols],
            v_ref[:, cols],
            (((0,), (0,)), ((), ())),
            preferred_element_type=jnp.float32,
        ).astype(s_ref.dtype)
    row_ids = lax.broadcasted_iota(jnp.int32, (rows, rows), 0)
    col_ids = lax.broadcasted_iota(jnp.int32, (rows, rows), 1)
    causal = col_ids <= row_ids
    copies[2].wait()
    copies[3].wait()
    for cols in heads:
        scores = lax.dot_general(
            q_ref[:, cols],
            k_ref[:, cols],
            (((1,), (1,)), ((), ())),
            preferred_element_type=jnp.float32,
        )
        scores = jnp.where(causal, scores, 0.0).astype(jnp.bfloat16)
        w_ref[:, cols] = jnp.dot(scores, v_ref[:, cols], preferred_element_type=jnp.float32)


def scan_kernel(a_ref, p_ref):
    total = jnp.zeros(a_ref.shape[1:], jnp.float32)
    for c in range(a_ref.shape[0]):
        p_ref[c] = total.astype(p_ref.dtype)
        total = total + a_ref[c].astype(jnp.float32)


def attend_kernel(q_ref, w_ref, p_ref, g_ref, o_ref):
    for h in range(0, q_ref.shape[1], DH):
        cols = slice(h, h + DH)
        attended = jnp.dot(q_ref[:, cols], p_ref[cols, :], preferred_element_type=jnp.float32)
        attended = attended + w_ref[:, cols]
        mean = jnp.mean(attended * attended, axis=-1, keepdims=True)
        o_ref[:, cols] = (attended * lax.rsqrt(mean + epsilon) * g_ref[...]).astype(o_ref.dtype)


def source(me, ring, step, other):
    core = lax.rem(me, 2)
    at = lax.div(me, 2) + jnp.where(core == 0, ring - step, step)
    return 2 * lax.rem(at, ring) + (1 - core if other else core)


def in_hbm(*arrays):
    return [pltpu.with_memory_space_constraint(a, pltpu.HBM) for a in arrays]


def fetch(weight_refs, rows, out_ref, sems):
    depth = out_ref.shape[1]
    copies = []
    for n, (w, block) in enumerate(rows):
        at = pl.multiple_of(block * depth, depth)
        source_rows = weight_refs[w].at[pl.ds(at, depth), :]
        copies.append(pltpu.make_async_copy(source_rows, out_ref.at[n], sems.at[n]))
        copies[-1].start()
    return copies


def wanted(me, ring, step, other):
    block = source(me, ring, step, other)
    if step <= (ring - 1) // 2:
        return [(0, block), (1, block)]
    chip = lax.div(block, 2)
    return [(0, 2 * chip), (0, 2 * chip + 1)]


def project_kernel(ring, here, then, first, me_ref, block_ref, w0_ref, w1_ref, *refs):
    me = me_ref[0]
    weights = (w0_ref, w1_ref)
    if first:
        outs, (ahead_ref, now_ref, sems, now_sems) = refs[:2], refs[2:]
        now = fetch(weights, wanted(me, ring, *here), now_ref, now_sems)
    else:
        now_ref, seeds, outs, (ahead_ref, sems) = refs[0], refs[1:3], refs[3:5], refs[5:]
    ahead = fetch(weights, wanted(me, ring, *then), ahead_ref, sems)
    for n in range(2):
        if first:
            now[n].wait()
        part = jnp.dot(block_ref[...], now_ref[n], preferred_element_type=jnp.float32)
        outs[n][...] = part if first else seeds[n][...] + part
    for copy in ahead:
        copy.wait()


def project(me, ring, here, then, block, columns, state):
    rows, depth = block.shape
    cols = columns[0].shape[1]
    dtype = columns[0].dtype
    first = state is None
    slots = (2, depth, cols)
    sums = [jax.ShapeDtypeStruct((rows, cols), jnp.float32)] * 2
    scratch = [pltpu.VMEM(slots, dtype)] if first else []
    scratch += [pltpu.SemaphoreType.DMA((2,))] * (2 if first else 1)
    mine, theirs, ahead = pl.pallas_call(
        functools.partial(project_kernel, ring, here, then, first),
        out_shape=sums + [jax.ShapeDtypeStruct(slots, dtype)],
        in_specs=[SMEM, VMEM, HBM, HBM] + ([] if first else [VMEM] * 3),
        out_specs=[VMEM] * 3,
        scratch_shapes=scratch,
        compiler_params=PARAMS,
        cost_estimate=pl.CostEstimate(
            flops=4 * rows * depth * cols,
            bytes_accessed=2 * depth * cols * 2,
            transcendentals=0,
        ),
    )(me.reshape(1), block, *in_hbm(*columns), *(() if first else state))
    return ahead, mine, theirs


def pair_kernel(pair_ref, w_ref, mine_ref, back_ref, out_ref):
    rows = mine_ref.shape[0]
    total = mine_ref[...] + back_ref[...]
    for n in range(2):
        block = pair_ref[n * rows : (n + 1) * rows, :]
        total = total + jnp.dot(block, w_ref[n], preferred_element_type=jnp.float32)
    out_ref[...] = total.astype(out_ref.dtype)


def call(kernel, shape, dtype, args, flops):
    size = sum(a.size * a.dtype.itemsize for a in args)
    return pl.pallas_call(
        kernel,
        out_shape=jax.ShapeDtypeStruct(shape, dtype),
        in_specs=[VMEM] * len(args),
        out_specs=VMEM,
        compiler_params=PARAMS,
        cost_estimate=pl.CostEstimate(flops=flops, bytes_accessed=size, transcendentals=0),
    )(*args)


def local(queries, keys, values, gain):
    rows, width = queries.shape
    return pl.pallas_call(
        local_kernel,
        out_shape=[
            jax.ShapeDtypeStruct((width, DH), jnp.bfloat16),
            jax.ShapeDtypeStruct((rows, width), jnp.float32),
            jax.ShapeDtypeStruct((rows, width), queries.dtype),
            jax.ShapeDtypeStruct(gain.shape, gain.dtype),
        ],
        in_specs=[HBM] * 4,
        out_specs=[VMEM] * 4,
        scratch_shapes=[
            pltpu.VMEM((rows, width), keys.dtype),
            pltpu.VMEM((rows, width), values.dtype),
            pltpu.SemaphoreType.DMA((4,)),
        ],
        compiler_params=PARAMS,
        cost_estimate=pl.CostEstimate(
            flops=2 * rows * width * (DH + 2 * rows),
            bytes_accessed=3 * rows * width * 2,
            transcendentals=0,
        ),
    )(*in_hbm(queries, keys, values, gain))


def on_device(queries, keys, values, norm_gain, out_weight):
    rows, width = queries.shape
    groups = lax.axis_size("seq")
    tp = lax.axis_size("tp")
    ring = tp // 2
    me = lax.axis_index("tp")
    partner = [(j, j ^ 1) for j in range(tp)]
    onward = [
        (2 * y + c, 2 * ((y + (1, -1)[c]) % ring) + c) for y in range(ring) for c in range(2)
    ]
    across = [(s ^ 1, d) for s, d in onward]
    tie = lax.optimization_barrier

    states, within, near_queries, gain = local(
        queries, keys, values, norm_gain.reshape(1, DH)
    )
    weight, states = tie((out_weight, states))
    columns = (out_weight, lax.ppermute(weight, "tp", partner))
    slices = states.reshape(groups, width // groups, DH)
    slices = lax.all_to_all(slices, "seq", 0, 0, tiled=True)
    prefix = call(scan_kernel, slices.shape, jnp.bfloat16, (slices,), slices.size)
    prefix = lax.all_to_all(prefix, "seq", 0, 0, tiled=True).reshape(width, DH)
    own = call(
        attend_kernel,
        (rows, width),
        jnp.bfloat16,
        (near_queries, within, prefix, gain),
        2 * rows * width * DH,
    )

    halves = [[2 * y, 2 * y + 1] for y in range(ring)]
    half = (ring - 1) // 2

    def send(block, pairs):
        return lax.ppermute(block, "tp", pairs)

    def multiply(here, then, block, state):
        return project(me, ring, here, then, block, columns, state)

    first = send(own, onward)
    second = send(own, across)
    state = multiply((0, False), (1, False), own, None)
    for step in range(1, half + 1):
        first, state = tie((first, state))
        state = multiply((step, False), (step, True), first, state)
        first = send(first, onward)
        second, state = tie((second, state))
        state = multiply((step, True), (step + 1, False), second, state)
        if step < half:
            second = send(second, onward)
    ahead, mine, theirs = state
    returned = send(theirs, partner)
    first, returned = tie((first, returned))
    pair = lax.all_gather(first, "tp", axis=0, tiled=True, axis_index_groups=halves)
    return call(
        pair_kernel,
        (rows, width),
        jnp.bfloat16,
        (pair, ahead, mine, returned),
        4 * rows * width * width,
    )


def solution(mesh):
    return jax.shard_map(
        on_device,
        mesh=mesh,
        in_specs=(P("seq", "tp"), P("seq", "tp"), P("seq", "tp"), P(), P(None, "tp")),
        out_specs=P("seq", "tp"),
        check_vma=False,
    )
```

time: 121 us -> 117 us (0.967)
  local copies, waits for them, and re-layouts: 3.5 us -> 0 us
    unnamed x8 -> x0, local copies, waits for them, and re-layouts: 3.5 us -> none
    pallas_call x8 -> x7, Pallas kernels: 14 us -> 10.9 us  [project(): pl.pallas_call(functools.partial(project_kernel, ring, here, then, first)...]
    pallas_call x1, Pallas kernels: 0.64 us -> 1.88 us  [local(): pl.pallas_call(local_kernel, out_shape=[jax.ShapeDtypeStruct((width, DH),...]
  transfers between devices with their start and end apart: 9 -> 9, of which waited for: 2 -> 2; matrix products, arithmetic and copies ran while one was open for 0% -> 0% of each run, Pallas kernels for 9% -> 8%
where the time goes in v1:
time: 117 us; the launch traced here: 116 us
  blocking collectives  48 us (41%)
  starting transfers between devices  46.5 us (40%)
  Pallas kernels  14.3 us (12%)
  waiting for transfers between devices  7.16 us (6%)
    ppermute x8, starting transfers between devices, send(): return lax.ppermute(block, 'tp', pairs)  30.5 us
    all_to_all x1, blocking collectives, on_device(): slices = lax.all_to_all(slices, 'seq', 0, 0, tiled=True)  24 us
    all_to_all x1, blocking collectives, on_device(): prefix = lax.all_to_all(prefix, 'seq', 0, 0, tiled=True).reshape(width, DH)  20.9 us
    ppermute x1, starting transfers between devices, on_device(): columns = (out_weight, lax.ppermute(weight, 'tp', partner))  16 us
    pallas_call x7, Pallas kernels, project(): pl.pallas_call(functools.partial(project_kernel, ring, here, then, first)...  10.9 us
    ppermute x8, waiting for transfers between devices, send(): return lax.ppermute(block, 'tp', pairs)  7.15 us
    all_gather x1, blocking collectives, on_device(): lax.all_gather(first, 'tp', axis=0, tiled=True, axis_index_groups=halves)  3.13 us
  transfers between devices with their start and end apart: 9, of which 2 were waited for; matrix products, arithmetic and copies ran while one was open for 0% of the time, Pallas kernels for 8%

profile of v1, /device:TPU:1, one launch (start us, length us, event | category | flops | bytes accessed | tf_op | source)
XLA Modules:
  0.0 116.2 jit_solution(2593094128650302933)
XLA Ops:
  0.0 1.9 %shard_map.55 = (bf16[512,128]{1,0:T(8,128)(2,1)S(1)}, f32[256,512]{1,0:T(8,128)S(1)}, bf16[256,512]{1,0:T(8,128)(2,1)S(1)}, f32[1,128]{1,0:T(1,128)S(1)}) custom-call(bf16[256,512]{1,0:T(8,128)(2,1)} %q_hbm.1, bf16[256,512]{1,0:T(8,128)(2,1)} %k_hbm.1, bf16[256,512]{1,0:T(8,128)(2,1)} %v_hbm.1, f32[1,128]{1,0:T(1,128)} %bitcast.6), custom_call_target="tpu_custom_call" | custom-call | flops 167772160 | bytes 786432 | tf_op jit(solution)/shard_map/pallas_call | solution.py:164
  1.9 16.0 %collective-permute-start.1 = (bf16[8192,512]{1,0:T(8,128)(2,1)}, bf16[8192,512]{1,0:T(8,128)(2,1)}, u32[]{:S(2)}, u32[]{:S(2)}) collective-permute-start(bf16[8192,512]{1,0:T(8,128)(2,1)} %w0_ref.13), channel_id=1, source_target_pairs={{0,1},{1,0},{2,3},{3,2},{4,5},{5,4},{6,7},{7,6},{8,9},{9,8},{10,11... | collective-permute-start | bytes 25165832 | tf_op jit(solution)/shard_map/ppermute | solution.py:205
  17.9 24.0 %all_to_all.10.a_ref = bf16[64,8,128]{2,1,0:T(8,128)(2,1)S(1)} all-to-all(bf16[64,8,128]{2,1,0:T(8,128)(2,1)S(1)} %bitcast.5), channel_id=1, replica_groups=mesh['seq'=64,'tp'=16] {'seq'}, dimensions={0} | all-to-all | bytes 262144 | tf_op jit(solution)/shard_map/all_to_all | solution.py:207
  42.0 0.1 shard_map.56
  42.0 20.9 %all_to_all.11 = bf16[64,8,128]{2,1,0:T(8,128)(2,1)S(1)} all-to-all(bf16[64,8,128]{2,1,0:T(8,128)(2,1)S(1)} %shard_map.56), channel_id=1, replica_groups=mesh['seq'=64,'tp'=16] {'seq'}, dimensions={0} | all-to-all | bytes 262144 | tf_op jit(solution)/shard_map/all_to_all | solution.py:209
  62.9 0.4 shard_map.57.block_ref
  63.3 5.1 %collective-permute-start = (bf16[256,512]{1,0:T(8,128)(2,1)S(1)}, bf16[256,512]{1,0:T(8,128)(2,1)S(1)}, u32[]{:S(2)}, u32[]{:S(2)}) collective-permute-start(bf16[256,512]{1,0:T(8,128)(2,1)S(1)} %shard_map.57.block_ref), channel_id=1, source_target_pairs={{0,2},{1,15},{2,4},{3,1},{4,6},{5,3},{6,8},{7,5},{8,10},{9,7},{10,... | collective-permute-start | bytes 786440 | tf_op jit(solution)/shard_map/ppermute | solution.py:222
  68.4 4.6 %collective-permute-start.3 = (bf16[256,512]{1,0:T(8,128)(2,1)S(1)}, bf16[256,512]{1,0:T(8,128)(2,1)S(1)}, u32[]{:S(2)}, u32[]{:S(2)}) collective-permute-start(bf16[256,512]{1,0:T(8,128)(2,1)S(1)} %shard_map.57.block_ref), channel_id=1, source_target_pairs={{1,2},{0,15},{3,4},{2,1},{5,6},{4,3},{7,8},{6,5},{9,10},{8,7},{11,... | collective-permute-start | bytes 786440 | tf_op jit(solution)/shard_map/ppermute | solution.py:222
  73.0 0.0 collective-permute-done.1.w1_ref
  73.0 1.7 %shard_map.58 = (f32[256,512]{1,0:T(8,128)S(1)}, f32[256,512]{1,0:T(8,128)S(1)}, bf16[2,512,512]{2,1,0:T(8,128)(2,1)S(1)}) custom-call(s32[1]{0:T(128)} %bitcast.3.me_ref, bf16[256,512]{1,0:T(8,128)(2,1)S(1)} %shard_map.57.block_ref, bf16[8192,512]{1,0:T(8,128)(2,1)} %w0_ref.13, bf16[8192,512]{1,0:T(8,128)(2,1)} %collective-permute-done.1.w1_ref), custom_call_target="tpu_custom_call" | custom-call | flops 268435456 | bytes 1048576 | tf_op jit(solution)/shard_map/pallas_call | solution.py:125
  74.7 0.0 collective-permute-done.block_ref
  74.7 3.3 %collective-permute-start.2 = (bf16[256,512]{1,0:T(8,128)(2,1)S(1)}, bf16[256,512]{1,0:T(8,128)(2,1)S(1)}, u32[]{:S(2)}, u32[]{:S(2)}) collective-permute-start(bf16[256,512]{1,0:T(8,128)(2,1)S(1)} %collective-permute-done.block_ref), channel_id=1, source_target_pairs={{0,2},{1,15},{2,4},{3,1},{4,6},{5,3},{6,8},{7,5},{8,10},{9,7},{10,... | collective-permute-start | bytes 786440 | tf_op jit(solution)/shard_map/ppermute | solution.py:222
  78.0 1.5 %shard_map.59 = (f32[256,512]{1,0:T(8,128)S(1)}, f32[256,512]{1,0:T(8,128)S(1)}, bf16[2,512,512]{2,1,0:T(8,128)(2,1)S(1)}) custom-call(s32[1]{0:T(128)} %bitcast.3.me_ref, bf16[256,512]{1,0:T(8,128)(2,1)S(1)} %collective-permute-done.block_ref, bf16[8192,512]{1,0:T(8,128)(2,1)} %w0_ref.13, bf16[8192,512]{1,0:T(8,128)(2,1)} %collective-permute-done.1.w1_ref, ...), custom_call_target="tpu_custom_call" | custom-call | flops 268435456 | bytes 1048576 | tf_op jit(solution)/shard_map/pallas_call | solution.py:125
  79.6 0.0 collective-permute-done.3.block_ref
  79.6 2.3 %collective-permute-start.5 = (bf16[256,512]{1,0:T(8,128)(2,1)S(1)}, bf16[256,512]{1,0:T(8,128)(2,1)S(1)}, u32[]{:S(2)}, u32[]{:S(2)}) collective-permute-start(bf16[256,512]{1,0:T(8,128)(2,1)S(1)} %collective-permute-done.3.block_ref), channel_id=1, source_target_pairs={{0,2},{1,15},{2,4},{3,1},{4,6},{5,3},{6,8},{7,5},{8,10},{9,7},{10,... | collective-permute-start | bytes 786440 | tf_op jit(solution)/shard_map/ppermute | solution.py:222
  81.9 1.5 %shard_map.60 = (f32[256,512]{1,0:T(8,128)S(1)}, f32[256,512]{1,0:T(8,128)S(1)}, bf16[2,512,512]{2,1,0:T(8,128)(2,1)S(1)}) custom-call(s32[1]{0:T(128)} %bitcast.3.me_ref, bf16[256,512]{1,0:T(8,128)(2,1)S(1)} %collective-permute-done.3.block_ref, bf16[8192,512]{1,0:T(8,128)(2,1)} %w0_ref.13, bf16[8192,512]{1,0:T(8,128)(2,1)} %collective-permute-done.1.w1_ref, ...), custom_call_target="tpu_custom_call" | custom-call | flops 268435456 | bytes 1048576 | tf_op jit(solution)/shard_map/pallas_call | solution.py:125
  83.4 0.0 collective-permute-done.2.block_ref
  83.5 3.6 %collective-permute-start.4 = (bf16[256,512]{1,0:T(8,128)(2,1)S(1)}, bf16[256,512]{1,0:T(8,128)(2,1)S(1)}, u32[]{:S(2)}, u32[]{:S(2)}) collective-permute-start(bf16[256,512]{1,0:T(8,128)(2,1)S(1)} %collective-permute-done.2.block_ref), channel_id=1, source_target_pairs={{0,2},{1,15},{2,4},{3,1},{4,6},{5,3},{6,8},{7,5},{8,10},{9,7},{10,... | collective-permute-start | bytes 786440 | tf_op jit(solution)/shard_map/ppermute | solution.py:222
  87.1 1.5 %shard_map.61 = (f32[256,512]{1,0:T(8,128)S(1)}, f32[256,512]{1,0:T(8,128)S(1)}, bf16[2,512,512]{2,1,0:T(8,128)(2,1)S(1)}) custom-call(s32[1]{0:T(128)} %bitcast.3.me_ref, bf16[256,512]{1,0:T(8,128)(2,1)S(1)} %collective-permute-done.2.block_ref, bf16[8192,512]{1,0:T(8,128)(2,1)} %w0_ref.13, bf16[8192,512]{1,0:T(8,128)(2,1)} %collective-permute-done.1.w1_ref, ...), custom_call_target="tpu_custom_call" | custom-call | flops 268435456 | bytes 1048576 | tf_op jit(solution)/shard_map/pallas_call | solution.py:125
  88.6 0.0 collective-permute-done.5.block_ref
  88.6 3.0 %collective-permute-start.7 = (bf16[256,512]{1,0:T(8,128)(2,1)S(1)}, bf16[256,512]{1,0:T(8,128)(2,1)S(1)}, u32[]{:S(2)}, u32[]{:S(2)}) collective-permute-start(bf16[256,512]{1,0:T(8,128)(2,1)S(1)} %collective-permute-done.5.block_ref), channel_id=1, source_target_pairs={{0,2},{1,15},{2,4},{3,1},{4,6},{5,3},{6,8},{7,5},{8,10},{9,7},{10,... | collective-permute-start | bytes 786440 | tf_op jit(solution)/shard_map/ppermute | solution.py:222
  91.6 1.5 %shard_map.62 = (f32[256,512]{1,0:T(8,128)S(1)}, f32[256,512]{1,0:T(8,128)S(1)}, bf16[2,512,512]{2,1,0:T(8,128)(2,1)S(1)}) custom-call(s32[1]{0:T(128)} %bitcast.3.me_ref, bf16[256,512]{1,0:T(8,128)(2,1)S(1)} %collective-permute-done.5.block_ref, bf16[8192,512]{1,0:T(8,128)(2,1)} %w0_ref.13, bf16[8192,512]{1,0:T(8,128)(2,1)} %collective-permute-done.1.w1_ref, ...), custom_call_target="tpu_custom_call" | custom-call | flops 268435456 | bytes 1048576 | tf_op jit(solution)/shard_map/pallas_call | solution.py:125
  93.2 0.0 collective-permute-done.4.block_ref
  93.2 1.5 %shard_map.63 = (f32[256,512]{1,0:T(8,128)S(1)}, f32[256,512]{1,0:T(8,128)S(1)}, bf16[2,512,512]{2,1,0:T(8,128)(2,1)S(1)}) custom-call(s32[1]{0:T(128)} %bitcast.3.me_ref, bf16[256,512]{1,0:T(8,128)(2,1)S(1)} %collective-permute-done.4.block_ref, bf16[8192,512]{1,0:T(8,128)(2,1)} %w0_ref.13, bf16[8192,512]{1,0:T(8,128)(2,1)} %collective-permute-done.1.w1_ref, ...), custom_call_target="tpu_custom_call" | custom-call | flops 268435456 | bytes 1048576 | tf_op jit(solution)/shard_map/pallas_call | solution.py:125
  94.7 1.1 collective-permute-done.7.block_ref
  95.8 1.5 %shard_map.64 = (f32[256,512]{1,0:T(8,128)S(1)}, f32[256,512]{1,0:T(8,128)S(1)}, bf16[2,512,512]{2,1,0:T(8,128)(2,1)S(1)}) custom-call(s32[1]{0:T(128)} %bitcast.3.me_ref, bf16[256,512]{1,0:T(8,128)(2,1)S(1)} %collective-permute-done.7.block_ref, bf16[8192,512]{1,0:T(8,128)(2,1)} %w0_ref.13, bf16[8192,512]{1,0:T(8,128)(2,1)} %collective-permute-done.1.w1_ref, ...), custom_call_target="tpu_custom_call" | custom-call | flops 268435456 | bytes 1048576 | tf_op jit(solution)/shard_map/pallas_call | solution.py:125
  97.3 6.5 %collective-permute-start.8 = (f32[256,512]{1,0:T(8,128)S(1)}, f32[256,512]{1,0:T(8,128)S(1)}, u32[]{:S(2)}, u32[]{:S(2)}) collective-permute-start(f32[256,512]{1,0:T(8,128)S(1)} %get-tuple-element.106), channel_id=1, source_target_pairs={{0,1},{1,0},{2,3},{3,2},{4,5},{5,4},{6,7},{7,6},{8,9},{9,8},{10,11... | collective-permute-start | bytes 1572872 | tf_op jit(solution)/shard_map/ppermute | solution.py:222
  103.8 2.1 %collective-permute-start.6 = (bf16[256,512]{1,0:T(8,128)(2,1)S(1)}, bf16[256,512]{1,0:T(8,128)(2,1)S(1)}, u32[]{:S(2)}, u32[]{:S(2)}) collective-permute-start(bf16[256,512]{1,0:T(8,128)(2,1)S(1)} %collective-permute-done.4.block_ref), channel_id=1, source_target_pairs={{0,2},{1,15},{2,4},{3,1},{4,6},{5,3},{6,8},{7,5},{8,10},{9,7},{10,... | collective-permute-start | bytes 786440 | tf_op jit(solution)/shard_map/ppermute | solution.py:222
  105.9 6.1 %collective-permute-done.6 = bf16[256,512]{1,0:T(8,128)(2,1)S(1)} collective-permute-done((bf16[256,512]{1,0:T(8,128)(2,1)S(1)}, bf16[256,512]{1,0:T(8,128)(2,1)S(1)}, u32[]{:S(2)}, u32[]{:S(2)}) %collective-permute-start.6) | collective-permute-done | bytes 262176 | tf_op jit(solution)/shard_map/ppermute | solution.py:222
  112.0 0.0 collective-permute-done.8.back_ref
  112.0 3.1 %all_gather.3.pair_ref = bf16[512,512]{1,0:T(8,128)(2,1)S(1)} all-gather(bf16[256,512]{1,0:T(8,128)(2,1)S(1)} %collective-permute-done.6), channel_id=1, replica_groups={{0,1},{2,3},{4,5},{6,7},{8,9},{10,11},{12,13},{14,15},{16,17},{18,19},{..., dimensions={0}, use_global_device_ids=true | all-gather | bytes 786432 | tf_op jit(solution)/shard_map/all_gather | solution.py:241
  115.1 1.2 shard_map.65
Async XLA Ops:
  1.9 71.1 %collective-permute-start.1 = (bf16[8192,512]{1,0:T(8,128)(2,1)}, bf16[8192,512]{1,0:T(8,128)(2,1)}, u32[]{:S(2)}, u32[]{:S(2)}) collective-permute-start(bf16[8192,512]{1,0:T(8,128)(2,1)} %w0_ref.13), channel_id=1, source_target_pairs={{0,1},{1,0},{2,3},{3,2},{4,5},{5,4},{6,7},{7,6},{8,9},{9,8},{10,11... | collective-permute-start | bytes 25165832 | tf_op jit(solution)/shard_map/ppermute | solution.py:205
  63.3 11.4 %collective-permute-start = (bf16[256,512]{1,0:T(8,128)(2,1)S(1)}, bf16[256,512]{1,0:T(8,128)(2,1)S(1)}, u32[]{:S(2)}, u32[]{:S(2)}) collective-permute-start(bf16[256,512]{1,0:T(8,128)(2,1)S(1)} %shard_map.57.block_ref), channel_id=1, source_target_pairs={{0,2},{1,15},{2,4},{3,1},{4,6},{5,3},{6,8},{7,5},{8,10},{9,7},{10,... | collective-permute-start | bytes 786440 | tf_op jit(solution)/shard_map/ppermute | solution.py:222
  68.4 11.2 %collective-permute-start.3 = (bf16[256,512]{1,0:T(8,128)(2,1)S(1)}, bf16[256,512]{1,0:T(8,128)(2,1)S(1)}, u32[]{:S(2)}, u32[]{:S(2)}) collective-permute-start(bf16[256,512]{1,0:T(8,128)(2,1)S(1)} %shard_map.57.block_ref), channel_id=1, source_target_pairs={{1,2},{0,15},{3,4},{2,1},{5,6},{4,3},{7,8},{6,5},{9,10},{8,7},{11,... | collective-permute-start | bytes 786440 | tf_op jit(solution)/shard_map/ppermute | solution.py:222
  74.7 8.7 %collective-permute-start.2 = (bf16[256,512]{1,0:T(8,128)(2,1)S(1)}, bf16[256,512]{1,0:T(8,128)(2,1)S(1)}, u32[]{:S(2)}, u32[]{:S(2)}) collective-permute-start(bf16[256,512]{1,0:T(8,128)(2,1)S(1)} %collective-permute-done.block_ref), channel_id=1, source_target_pairs={{0,2},{1,15},{2,4},{3,1},{4,6},{5,3},{6,8},{7,5},{8,10},{9,7},{10,... | collective-permute-start | bytes 786440 | tf_op jit(solution)/shard_map/ppermute | solution.py:222
  79.6 9.1 %collective-permute-start.5 = (bf16[256,512]{1,0:T(8,128)(2,1)S(1)}, bf16[256,512]{1,0:T(8,128)(2,1)S(1)}, u32[]{:S(2)}, u32[]{:S(2)}) collective-permute-start(bf16[256,512]{1,0:T(8,128)(2,1)S(1)} %collective-permute-done.3.block_ref), channel_id=1, source_target_pairs={{0,2},{1,15},{2,4},{3,1},{4,6},{5,3},{6,8},{7,5},{8,10},{9,7},{10,... | collective-permute-start | bytes 786440 | tf_op jit(solution)/shard_map/ppermute | solution.py:222
  83.5 9.7 %collective-permute-start.4 = (bf16[256,512]{1,0:T(8,128)(2,1)S(1)}, bf16[256,512]{1,0:T(8,128)(2,1)S(1)}, u32[]{:S(2)}, u32[]{:S(2)}) collective-permute-start(bf16[256,512]{1,0:T(8,128)(2,1)S(1)} %collective-permute-done.2.block_ref), channel_id=1, source_target_pairs={{0,2},{1,15},{2,4},{3,1},{4,6},{5,3},{6,8},{7,5},{8,10},{9,7},{10,... | collective-permute-start | bytes 786440 | tf_op jit(solution)/shard_map/ppermute | solution.py:222
  88.6 7.1 %collective-permute-start.7 = (bf16[256,512]{1,0:T(8,128)(2,1)S(1)}, bf16[256,512]{1,0:T(8,128)(2,1)S(1)}, u32[]{:S(2)}, u32[]{:S(2)}) collective-permute-start(bf16[256,512]{1,0:T(8,128)(2,1)S(1)} %collective-permute-done.5.block_ref), channel_id=1, source_target_pairs={{0,2},{1,15},{2,4},{3,1},{4,6},{5,3},{6,8},{7,5},{8,10},{9,7},{10,... | collective-permute-start | bytes 786440 | tf_op jit(solution)/shard_map/ppermute | solution.py:222
  97.3 14.7 %collective-permute-start.8 = (f32[256,512]{1,0:T(8,128)S(1)}, f32[256,512]{1,0:T(8,128)S(1)}, u32[]{:S(2)}, u32[]{:S(2)}) collective-permute-start(f32[256,512]{1,0:T(8,128)S(1)} %get-tuple-element.106), channel_id=1, source_target_pairs={{0,1},{1,0},{2,3},{3,2},{4,5},{5,4},{6,7},{7,6},{8,9},{9,8},{10,11... | collective-permute-start | bytes 1572872 | tf_op jit(solution)/shard_map/ppermute | solution.py:222
  103.8 8.2 %collective-permute-start.6 = (bf16[256,512]{1,0:T(8,128)(2,1)S(1)}, bf16[256,512]{1,0:T(8,128)(2,1)S(1)}, u32[]{:S(2)}, u32[]{:S(2)}) collective-permute-start(bf16[256,512]{1,0:T(8,128)(2,1)S(1)} %collective-permute-done.4.block_ref), channel_id=1, source_target_pairs={{0,2},{1,15},{2,4},{3,1},{4,6},{5,3},{6,8},{7,5},{8,10},{9,7},{10,... | collective-permute-start | bytes 786440 | tf_op jit(solution)/shard_map/ppermute | solution.py:222

commit v2 on v1

--- a/solution.py
+++ b/solution.py
@@ -66,9 +66,9 @@
         o_ref[:, cols] = (attended * lax.rsqrt(mean + epsilon) * g_ref[...]).astype(o_ref.dtype)
 
 
-def source(me, ring, step, other):
-    core = lax.rem(me, 2)
-    at = lax.div(me, 2) + jnp.where(core == 0, ring - step, step)
+def source(me, ring, step, other, core=None):
+    core = lax.rem(me, 2) if core is None else core
+    at = lax.div(me, 2) + (jnp.where(core == 0, ring - step, step))
     return 2 * lax.rem(at, ring) + (1 - core if other else core)
 
 
@@ -87,64 +87,69 @@
     return copies
 
 
-def wanted(me, ring, step, other):
-    block = source(me, ring, step, other)
-    if step <= (ring - 1) // 2:
-        return [(0, block), (1, block)]
-    chip = lax.div(block, 2)
-    return [(0, 2 * chip), (0, 2 * chip + 1)]
-
-
-def project_kernel(ring, here, then, first, me_ref, block_ref, w0_ref, w1_ref, *refs):
-    me = me_ref[0]
-    weights = (w0_ref, w1_ref)
-    if first:
-        outs, (ahead_ref, now_ref, sems, now_sems) = refs[:2], refs[2:]
-        now = fetch(weights, wanted(me, ring, *here), now_ref, now_sems)
-    else:
-        now_ref, seeds, outs, (ahead_ref, sems) = refs[0], refs[1:3], refs[3:5], refs[5:]
-    ahead = fetch(weights, wanted(me, ring, *then), ahead_ref, sems)
+def add_products(block_ref, rows_ref, slot, seeds, outs):
     for n in range(2):
-        if first:
-            now[n].wait()
-        part = jnp.dot(block_ref[...], now_ref[n], preferred_element_type=jnp.float32)
-        outs[n][...] = part if first else seeds[n][...] + part
+        part = jnp.dot(block_ref[...], rows_ref[slot + n], preferred_element_type=jnp.float32)
+        outs[n][...] = seeds[n][...] + part if seeds else part
+
+
+def first_kernel(ring, later, me_ref, block_ref, w0_ref, w1_ref, *refs):
+    mine_ref, theirs_ref, ahead_ref, now_ref, now_sems, sems = refs
+    me, weights = me_ref[0], (w0_ref, w1_ref)
+    now = fetch(weights, [(n, me) for n in range(2)], now_ref, now_sems)
+    rows = [(n, source(me, ring, *item)) for item in later for n in range(2)]
+    ahead = fetch(weights, rows, ahead_ref, sems)
+    for copy in now:
+        copy.wait()
+    add_products(block_ref, now_ref, 0, None, (mine_ref, theirs_ref))
     for copy in ahead:
         copy.wait()
 
 
-def project(me, ring, here, then, block, columns, state):
+def next_kernel(slot, block_ref, rows_ref, *refs):
+    add_products(block_ref, rows_ref, slot, refs[:2], refs[2:])
+
+
+def last_kernel(ring, slot, final, me_ref, block_ref, rows_ref, m_ref, t_ref, w_ref, *refs):
+    mine_ref, theirs_ref, ahead_ref, sems = refs
+    rows = [(0, source(me_ref[0], ring, *item)) for item in final]
+    ahead = fetch((w_ref,), rows, ahead_ref, sems)
+    add_products(block_ref, rows_ref, slot, (m_ref, t_ref), (mine_ref, theirs_ref))
+    for copy in ahead:
+        copy.wait()
+
+
+def output_kernel(near_ref, far_ref, w_ref, mine_ref, back_ref, out_ref):
+    rows = mine_ref.shape[0]
+    total = mine_ref[...] + back_ref[...]
+    for n in range(4):
+        pair_ref = (near_ref, far_ref)[n // 2]
+        block = pair_ref[n % 2 * rows : (n % 2 + 1) * rows, :]
+        total = total + jnp.dot(block, w_ref[n], preferred_element_type=jnp.float32)
+    out_ref[...] = total.astype(out_ref.dtype)
+
+
+def project(kernel, block, columns, fetched, operands, specs, scratch):
     rows, depth = block.shape
     cols = columns[0].shape[1]
     dtype = columns[0].dtype
-    first = state is None
-    slots = (2, depth, cols)
-    sums = [jax.ShapeDtypeStruct((rows, cols), jnp.float32)] * 2
-    scratch = [pltpu.VMEM(slots, dtype)] if first else []
-    scratch += [pltpu.SemaphoreType.DMA((2,))] * (2 if first else 1)
-    mine, theirs, ahead = pl.pallas_call(
-        functools.partial(project_kernel, ring, here, then, first),
-        out_shape=sums + [jax.ShapeDtypeStruct(slots, dtype)],
-        in_specs=[SMEM, VMEM, HBM, HBM] + ([] if first else [VMEM] * 3),
-        out_specs=[VMEM] * 3,
+    outs = [jax.ShapeDtypeStruct((rows, cols), jnp.float32)] * 2
+    if fetched:
+        outs.append(jax.ShapeDtypeStruct((fetched, depth, cols), dtype))
+        scratch = scratch + [pltpu.SemaphoreType.DMA((fetched,))]
+    return pl.pallas_call(
+        kernel,
+        out_shape=outs,
+        in_specs=specs,
+        out_specs=[VMEM] * len(outs),
         scratch_shapes=scratch,
         compiler_params=PARAMS,
         cost_estimate=pl.CostEstimate(
             flops=4 * rows * depth * cols,
-            bytes_accessed=2 * depth * cols * 2,
+            bytes_accessed=(2 + fetched) * depth * cols * 2,
             transcendentals=0,
         ),
-    )(me.reshape(1), block, *in_hbm(*columns), *(() if first else state))
-    return ahead, mine, theirs
-
-
-def pair_kernel(pair_ref, w_ref, mine_ref, back_ref, out_ref):
-    rows = mine_ref.shape[0]
-    total = mine_ref[...] + back_ref[...]
-    for n in range(2):
-        block = pair_ref[n * rows : (n + 1) * rows, :]
-        total = total + jnp.dot(block, w_ref[n], preferred_element_type=jnp.float32)
-    out_ref[...] = total.astype(out_ref.dtype)
+    )(*operands)
 
 
 def call(kernel, shape, dtype, args, flops):
@@ -195,6 +200,9 @@
     onward = [
         (2 * y + c, 2 * ((y + (1, -1)[c]) % ring) + c) for y in range(ring) for c in range(2)
     ]
+    onward_two = [
+        (2 * y + c, 2 * ((y + (2, -2)[c]) % ring) + c) for y in range(ring) for c in range(2)
+    ]
     across = [(s ^ 1, d) for s, d in onward]
     tie = lax.optimization_barrier
 
@@ -216,35 +224,70 @@
     )
 
     halves = [[2 * y, 2 * y + 1] for y in range(ring)]
-    half = (ring - 1) // 2
+    spot = me.reshape(1)
+    order = ((1, True), (1, False), (2, False), (2, True), (3, False))
+    final = ((3, True, 0), (3, True, 1), (4, False, 0), (4, False, 1))
 
     def send(block, pairs):
         return lax.ppermute(block, "tp", pairs)
 
-    def multiply(here, then, block, state):
-        return project(me, ring, here, then, block, columns, state)
-
-    first = send(own, onward)
-    second = send(own, across)
-    state = multiply((0, False), (1, False), own, None)
-    for step in range(1, half + 1):
-        first, state = tie((first, state))
-        state = multiply((step, False), (step, True), first, state)
-        first = send(first, onward)
-        second, state = tie((second, state))
-        state = multiply((step, True), (step + 1, False), second, state)
-        if step < half:
-            second = send(second, onward)
-    ahead, mine, theirs = state
+    def share(block):
+        return lax.all_gather(block, "tp", axis=0, tiled=True, axis_index_groups=halves)
+
+    def multiply(slot, block, ahead, sums):
+        return project(
+            functools.partial(next_kernel, 2 * slot),
+            block,
+            columns,
+            0,
+            (block, ahead, *sums),
+            [VMEM] * 4,
+            [],
+        )
+
+    b1 = send(own, across)
+    a2 = send(own, onward_two)
+    a1 = send(own, onward)
+    now = (2, width, out_weight.shape[1])
+    *sums, ahead = project(
+        functools.partial(first_kernel, ring, order),
+        own,
+        columns,
+        2 * len(order),
+        (spot, own, *in_hbm(*columns)),
+        [SMEM, VMEM, HBM, HBM],
+        [pltpu.VMEM(now, out_weight.dtype), pltpu.SemaphoreType.DMA((2,))],
+    )
+    b1, sums = tie((b1, sums))
+    b2 = send(b1, onward)
+    sums = multiply(0, b1, ahead, sums)
+    sums = multiply(1, a1, ahead, sums)
+    a2, sums = tie((a2, sums))
+    a4 = send(a2, onward_two)
+    a3 = send(a2, onward)
+    sums = multiply(2, a2, ahead, sums)
+    b2, sums = tie((b2, sums))
+    b3 = send(b2, onward)
+    sums = multiply(3, b2, ahead, sums)
+    mine, theirs, rest = project(
+        functools.partial(last_kernel, ring, 8, final),
+        a3,
+        columns,
+        len(final),
+        (spot, a3, ahead, *sums, *in_hbm(out_weight)),
+        [SMEM, VMEM, VMEM, VMEM, VMEM, HBM],
+        [],
+    )
     returned = send(theirs, partner)
-    first, returned = tie((first, returned))
-    pair = lax.all_gather(first, "tp", axis=0, tiled=True, axis_index_groups=halves)
+    near = share(b3)
+    a4, near = tie((a4, near))
+    far = share(a4)
     return call(
-        pair_kernel,
+        output_kernel,
         (rows, width),
         jnp.bfloat16,
-        (pair, ahead, mine, returned),
-        4 * rows * width * width,
+        (near, far, rest, mine, returned),
+        8 * rows * width * width,
     )
 
 

time: 117 us -> 115 us (0.983)
  Pallas kernels: 14.3 us -> 10.4 us
  blocking collectives: 48 us -> 50.9 us
  waiting for transfers between devices: 7.16 us -> 5.41 us
    pallas_call x7 -> x6, Pallas kernels: 10.9 us -> 6.65 us  [project(): pl.pallas_call(kernel, out_shape=outs, in_specs=specs, out_specs=[VMEM] *...]
    all_gather x1 -> x2, blocking collectives: 3.13 us -> 6 us  [share(): lax.all_gather(block, 'tp', axis=0, tiled=True, axis_index_groups=halves)]
    ppermute x8, waiting for transfers between devices: 7.15 us -> 5.41 us  [send(): return lax.ppermute(block, 'tp', pairs)]
  transfers between devices with their start and end apart: 9 -> 9, of which waited for: 2 -> 1; matrix products, arithmetic and copies ran while one was open for 0% -> 0% of each run, Pallas kernels for 8% -> 6%
where the time goes in v2:
time: 115 us; the launch traced here: 114 us
  blocking collectives  50.9 us (44%)
  starting transfers between devices  47.4 us (41%)
  Pallas kernels  10.4 us (9%)
  waiting for transfers between devices  5.41 us (5%)
    ppermute x8, starting transfers between devices, send(): return lax.ppermute(block, 'tp', pairs)  31.4 us
    all_to_all x1, blocking collectives, on_device(): slices = lax.all_to_all(slices, 'seq', 0, 0, tiled=True)  24 us
    all_to_all x1, blocking collectives, on_device(): prefix = lax.all_to_all(prefix, 'seq', 0, 0, tiled=True).reshape(width, DH)  20.9 us
    ppermute x1, starting transfers between devices, on_device(): columns = (out_weight, lax.ppermute(weight, 'tp', partner))  16 us
    pallas_call x6, Pallas kernels, project(): pl.pallas_call(kernel, out_shape=outs, in_specs=specs, out_specs=[VMEM] *...  6.65 us
    all_gather x2, blocking collectives, share(): lax.all_gather(block, 'tp', axis=0, tiled=True, axis_index_groups=halves)  6 us
    ppermute x8, waiting for transfers between devices, send(): return lax.ppermute(block, 'tp', pairs)  5.41 us
  transfers between devices with their start and end apart: 9, of which 1 were waited for; matrix products, arithmetic and copies ran while one was open for 0% of the time, Pallas kernels for 6%

profile of v2, /device:TPU:1, one launch (start us, length us, event | category | flops | bytes accessed | tf_op | source)
XLA Modules:
  0.0 114.3 jit_solution(17041756604901318217)
XLA Ops:
  0.0 1.9 %shard_map.55 = (bf16[512,128]{1,0:T(8,128)(2,1)S(1)}, f32[256,512]{1,0:T(8,128)S(1)}, bf16[256,512]{1,0:T(8,128)(2,1)S(1)}, f32[1,128]{1,0:T(1,128)S(1)}) custom-call(bf16[256,512]{1,0:T(8,128)(2,1)} %q_hbm.1, bf16[256,512]{1,0:T(8,128)(2,1)} %k_hbm.1, bf16[256,512]{1,0:T(8,128)(2,1)} %v_hbm.1, f32[1,128]{1,0:T(1,128)} %bitcast.6), custom_call_target="tpu_custom_call" | custom-call | flops 167772160 | bytes 786432 | tf_op jit(solution)/shard_map/pallas_call | solution.py:169
  1.9 16.0 %collective-permute-start.2 = (bf16[8192,512]{1,0:T(8,128)(2,1)}, bf16[8192,512]{1,0:T(8,128)(2,1)}, u32[]{:S(2)}, u32[]{:S(2)}) collective-permute-start(bf16[8192,512]{1,0:T(8,128)(2,1)} %w_ref.1), channel_id=1, source_target_pairs={{0,1},{1,0},{2,3},{3,2},{4,5},{5,4},{6,7},{7,6},{8,9},{9,8},{10,11... | collective-permute-start | bytes 25165832 | tf_op jit(solution)/shard_map/ppermute | solution.py:213
  17.9 24.0 %all_to_all.10.a_ref = bf16[64,8,128]{2,1,0:T(8,128)(2,1)S(1)} all-to-all(bf16[64,8,128]{2,1,0:T(8,128)(2,1)S(1)} %bitcast.5), channel_id=1, replica_groups=mesh['seq'=64,'tp'=16] {'seq'}, dimensions={0} | all-to-all | bytes 262144 | tf_op jit(solution)/shard_map/all_to_all | solution.py:215
  42.0 0.1 shard_map.56
  42.0 20.9 %all_to_all.11 = bf16[64,8,128]{2,1,0:T(8,128)(2,1)S(1)} all-to-all(bf16[64,8,128]{2,1,0:T(8,128)(2,1)S(1)} %shard_map.56), channel_id=1, replica_groups=mesh['seq'=64,'tp'=16] {'seq'}, dimensions={0} | all-to-all | bytes 262144 | tf_op jit(solution)/shard_map/all_to_all | solution.py:217
  62.9 0.4 shard_map.57.block_ref
  63.3 6.2 %collective-permute-start.3 = (bf16[256,512]{1,0:T(8,128)(2,1)S(1)}, bf16[256,512]{1,0:T(8,128)(2,1)S(1)}, u32[]{:S(2)}, u32[]{:S(2)}) collective-permute-start(bf16[256,512]{1,0:T(8,128)(2,1)S(1)} %shard_map.57.block_ref), channel_id=1, source_target_pairs={{1,2},{0,15},{3,4},{2,1},{5,6},{4,3},{7,8},{6,5},{9,10},{8,7},{11,... | collective-permute-start | bytes 786440 | tf_op jit(solution)/shard_map/ppermute | solution.py:232
  69.5 3.3 %collective-permute-start.1 = (bf16[256,512]{1,0:T(8,128)(2,1)S(1)}, bf16[256,512]{1,0:T(8,128)(2,1)S(1)}, u32[]{:S(2)}, u32[]{:S(2)}) collective-permute-start(bf16[256,512]{1,0:T(8,128)(2,1)S(1)} %shard_map.57.block_ref), channel_id=1, source_target_pairs={{0,2},{1,15},{2,4},{3,1},{4,6},{5,3},{6,8},{7,5},{8,10},{9,7},{10,... | collective-permute-start | bytes 786440 | tf_op jit(solution)/shard_map/ppermute | solution.py:232
  72.8 4.7 %collective-permute-start = (bf16[256,512]{1,0:T(8,128)(2,1)S(1)}, bf16[256,512]{1,0:T(8,128)(2,1)S(1)}, u32[]{:S(2)}, u32[]{:S(2)}) collective-permute-start(bf16[256,512]{1,0:T(8,128)(2,1)S(1)} %shard_map.57.block_ref), channel_id=1, source_target_pairs={{0,4},{1,13},{2,6},{3,15},{4,8},{5,1},{6,10},{7,3},{8,12},{9,5},{1... | collective-permute-start | bytes 786440 | tf_op jit(solution)/shard_map/ppermute | solution.py:232
  77.5 0.0 collective-permute-done.2.w1_ref
  77.5 3.0 %shard_map.58 = (f32[256,512]{1,0:T(8,128)S(1)}, f32[256,512]{1,0:T(8,128)S(1)}, bf16[10,512,512]{2,1,0:T(8,128)(2,1)S(1)}) custom-call(s32[1]{0:T(128)} %bitcast.3.me_ref, bf16[256,512]{1,0:T(8,128)(2,1)S(1)} %shard_map.57.block_ref, bf16[8192,512]{1,0:T(8,128)(2,1)} %w_ref.1, bf16[8192,512]{1,0:T(8,128)(2,1)} %collective-permute-done.2.w1_ref), custom_call_target="tpu_custom_call" | custom-call | flops 268435456 | bytes 6291456 | tf_op jit(solution)/shard_map/pallas_call | solution.py:140
  80.5 0.0 collective-permute-done.3.block_ref
  80.5 3.0 %collective-permute-start.5 = (bf16[256,512]{1,0:T(8,128)(2,1)S(1)}, bf16[256,512]{1,0:T(8,128)(2,1)S(1)}, u32[]{:S(2)}, u32[]{:S(2)}) collective-permute-start(bf16[256,512]{1,0:T(8,128)(2,1)S(1)} %collective-permute-done.3.block_ref), channel_id=1, source_target_pairs={{0,2},{1,15},{2,4},{3,1},{4,6},{5,3},{6,8},{7,5},{8,10},{9,7},{10,... | collective-permute-start | bytes 786440 | tf_op jit(solution)/shard_map/ppermute | solution.py:232
  83.5 0.4 shard_map.59
  84.0 0.0 collective-permute-done.1.block_ref
  84.0 0.4 shard_map.60
  84.4 0.0 collective-permute-done.block_ref
  84.4 4.2 %collective-permute-start.7 = (bf16[256,512]{1,0:T(8,128)(2,1)S(1)}, bf16[256,512]{1,0:T(8,128)(2,1)S(1)}, u32[]{:S(2)}, u32[]{:S(2)}) collective-permute-start(bf16[256,512]{1,0:T(8,128)(2,1)S(1)} %collective-permute-done.block_ref), channel_id=1, source_target_pairs={{0,2},{1,15},{2,4},{3,1},{4,6},{5,3},{6,8},{7,5},{8,10},{9,7},{10,... | collective-permute-start | bytes 786440 | tf_op jit(solution)/shard_map/ppermute | solution.py:232
  88.6 0.4 shard_map.61
  89.1 0.0 collective-permute-done.5.block_ref
  89.1 3.1 %collective-permute-start.6 = (bf16[256,512]{1,0:T(8,128)(2,1)S(1)}, bf16[256,512]{1,0:T(8,128)(2,1)S(1)}, u32[]{:S(2)}, u32[]{:S(2)}) collective-permute-start(bf16[256,512]{1,0:T(8,128)(2,1)S(1)} %collective-permute-done.5.block_ref), channel_id=1, source_target_pairs={{0,2},{1,15},{2,4},{3,1},{4,6},{5,3},{6,8},{7,5},{8,10},{9,7},{10,... | collective-permute-start | bytes 786440 | tf_op jit(solution)/shard_map/ppermute | solution.py:232
  92.2 0.4 shard_map.62
  92.6 0.0 collective-permute-done.7.block_ref
  92.6 1.9 %shard_map.63 = (f32[256,512]{1,0:T(8,128)S(1)}, f32[256,512]{1,0:T(8,128)S(1)}, bf16[4,512,512]{2,1,0:T(8,128)(2,1)S(1)}) custom-call(s32[1]{0:T(128)} %bitcast.3.me_ref, bf16[256,512]{1,0:T(8,128)(2,1)S(1)} %collective-permute-done.7.block_ref, bf16[10,512,512]{2,1,0:T(8,128)(2,1)S(1)} %get-tuple-element.42.rows_ref, ...), custom_call_target="tpu_custom_call" | custom-call | flops 268435456 | bytes 3145728 | tf_op jit(solution)/shard_map/pallas_call | solution.py:140
  94.5 3.8 %collective-permute-start.8 = (f32[256,512]{1,0:T(8,128)S(1)}, f32[256,512]{1,0:T(8,128)S(1)}, u32[]{:S(2)}, u32[]{:S(2)}) collective-permute-start(f32[256,512]{1,0:T(8,128)S(1)} %get-tuple-element.66), channel_id=1, source_target_pairs={{0,1},{1,0},{2,3},{3,2},{4,5},{5,4},{6,7},{7,6},{8,9},{9,8},{10,11... | collective-permute-start | bytes 1572872 | tf_op jit(solution)/shard_map/ppermute | solution.py:232
  98.3 3.2 %collective-permute-start.4 = (bf16[256,512]{1,0:T(8,128)(2,1)S(1)}, bf16[256,512]{1,0:T(8,128)(2,1)S(1)}, u32[]{:S(2)}, u32[]{:S(2)}) collective-permute-start(bf16[256,512]{1,0:T(8,128)(2,1)S(1)} %collective-permute-done.block_ref), channel_id=1, source_target_pairs={{0,4},{1,13},{2,6},{3,15},{4,8},{5,1},{6,10},{7,3},{8,12},{9,5},{1... | collective-permute-start | bytes 786440 | tf_op jit(solution)/shard_map/ppermute | solution.py:232
  101.5 0.0 collective-permute-done.6
  101.5 2.3 %all_gather.6.near_ref = bf16[512,512]{1,0:T(8,128)(2,1)S(1)} all-gather(bf16[256,512]{1,0:T(8,128)(2,1)S(1)} %collective-permute-done.6), channel_id=1, replica_groups={{0,1},{2,3},{4,5},{6,7},{8,9},{10,11},{12,13},{14,15},{16,17},{18,19},{..., dimensions={0}, use_global_device_ids=true | all-gather | bytes 786432 | tf_op jit(solution)/shard_map/all_gather | solution.py:235
  103.8 5.4 %collective-permute-done.4 = bf16[256,512]{1,0:T(8,128)(2,1)S(1)} collective-permute-done((bf16[256,512]{1,0:T(8,128)(2,1)S(1)}, bf16[256,512]{1,0:T(8,128)(2,1)S(1)}, u32[]{:S(2)}, u32[]{:S(2)}) %collective-permute-start.4) | collective-permute-done | bytes 262176 | tf_op jit(solution)/shard_map/ppermute | solution.py:232
  109.2 3.7 %all_gather.7.far_ref = bf16[512,512]{1,0:T(8,128)(2,1)S(1)} all-gather(bf16[256,512]{1,0:T(8,128)(2,1)S(1)} %collective-permute-done.4), channel_id=1, replica_groups={{0,1},{2,3},{4,5},{6,7},{8,9},{10,11},{12,13},{14,15},{16,17},{18,19},{..., dimensions={0}, use_global_device_ids=true | all-gather | bytes 786432 | tf_op jit(solution)/shard_map/all_gather | solution.py:235
  112.9 0.0 collective-permute-done.8.back_ref
  112.9 1.4 %shard_map.64 = bf16[256,512]{1,0:T(8,128)(2,1)} custom-call(bf16[512,512]{1,0:T(8,128)(2,1)S(1)} %all_gather.6.near_ref, bf16[512,512]{1,0:T(8,128)(2,1)S(1)} %all_gather.7.far_ref, bf16[4,512,512]{2,1,0:T(8,128)(2,1)S(1)} %get-tuple-element.64.w_ref, f32[256,512]{1,0:T(8,128)S(1)} %get-tuple-element.65.mine_ref, f32[256,512]{1,0:T(8,128)S(1)} %collective-permute-done.8.back_ref), custom_call_target="tpu_custom_call" | custom-call | flops 536870912 | bytes 4194304 | tf_op jit(solution)/shard_map/pallas_call | solution.py:157
Async XLA Ops:
  1.9 75.6 %collective-permute-start.2 = (bf16[8192,512]{1,0:T(8,128)(2,1)}, bf16[8192,512]{1,0:T(8,128)(2,1)}, u32[]{:S(2)}, u32[]{:S(2)}) collective-permute-start(bf16[8192,512]{1,0:T(8,128)(2,1)} %w_ref.1), channel_id=1, source_target_pairs={{0,1},{1,0},{2,3},{3,2},{4,5},{5,4},{6,7},{7,6},{8,9},{9,8},{10,11... | collective-permute-start | bytes 25165832 | tf_op jit(solution)/shard_map/ppermute | solution.py:213
  63.3 17.2 %collective-permute-start.3 = (bf16[256,512]{1,0:T(8,128)(2,1)S(1)}, bf16[256,512]{1,0:T(8,128)(2,1)S(1)}, u32[]{:S(2)}, u32[]{:S(2)}) collective-permute-start(bf16[256,512]{1,0:T(8,128)(2,1)S(1)} %shard_map.57.block_ref), channel_id=1, source_target_pairs={{1,2},{0,15},{3,4},{2,1},{5,6},{4,3},{7,8},{6,5},{9,10},{8,7},{11,... | collective-permute-start | bytes 786440 | tf_op jit(solution)/shard_map/ppermute | solution.py:232
  69.5 14.5 %collective-permute-start.1 = (bf16[256,512]{1,0:T(8,128)(2,1)S(1)}, bf16[256,512]{1,0:T(8,128)(2,1)S(1)}, u32[]{:S(2)}, u32[]{:S(2)}) collective-permute-start(bf16[256,512]{1,0:T(8,128)(2,1)S(1)} %shard_map.57.block_ref), channel_id=1, source_target_pairs={{0,2},{1,15},{2,4},{3,1},{4,6},{5,3},{6,8},{7,5},{8,10},{9,7},{10,... | collective-permute-start | bytes 786440 | tf_op jit(solution)/shard_map/ppermute | solution.py:232
  72.8 11.6 %collective-permute-start = (bf16[256,512]{1,0:T(8,128)(2,1)S(1)}, bf16[256,512]{1,0:T(8,128)(2,1)S(1)}, u32[]{:S(2)}, u32[]{:S(2)}) collective-permute-start(bf16[256,512]{1,0:T(8,128)(2,1)S(1)} %shard_map.57.block_ref), channel_id=1, source_target_pairs={{0,4},{1,13},{2,6},{3,15},{4,8},{5,1},{6,10},{7,3},{8,12},{9,5},{1... | collective-permute-start | bytes 786440 | tf_op jit(solution)/shard_map/ppermute | solution.py:232
  80.5 8.5 %collective-permute-start.5 = (bf16[256,512]{1,0:T(8,128)(2,1)S(1)}, bf16[256,512]{1,0:T(8,128)(2,1)S(1)}, u32[]{:S(2)}, u32[]{:S(2)}) collective-permute-start(bf16[256,512]{1,0:T(8,128)(2,1)S(1)} %collective-permute-done.3.block_ref), channel_id=1, source_target_pairs={{0,2},{1,15},{2,4},{3,1},{4,6},{5,3},{6,8},{7,5},{8,10},{9,7},{10,... | collective-permute-start | bytes 786440 | tf_op jit(solution)/shard_map/ppermute | solution.py:232
  84.4 8.2 %collective-permute-start.7 = (bf16[256,512]{1,0:T(8,128)(2,1)S(1)}, bf16[256,512]{1,0:T(8,128)(2,1)S(1)}, u32[]{:S(2)}, u32[]{:S(2)}) collective-permute-start(bf16[256,512]{1,0:T(8,128)(2,1)S(1)} %collective-permute-done.block_ref), channel_id=1, source_target_pairs={{0,2},{1,15},{2,4},{3,1},{4,6},{5,3},{6,8},{7,5},{8,10},{9,7},{10,... | collective-permute-start | bytes 786440 | tf_op jit(solution)/shard_map/ppermute | solution.py:232
  89.1 12.4 %collective-permute-start.6 = (bf16[256,512]{1,0:T(8,128)(2,1)S(1)}, bf16[256,512]{1,0:T(8,128)(2,1)S(1)}, u32[]{:S(2)}, u32[]{:S(2)}) collective-permute-start(bf16[256,512]{1,0:T(8,128)(2,1)S(1)} %collective-permute-done.5.block_ref), channel_id=1, source_target_pairs={{0,2},{1,15},{2,4},{3,1},{4,6},{5,3},{6,8},{7,5},{8,10},{9,7},{10,... | collective-permute-start | bytes 786440 | tf_op jit(solution)/shard_map/ppermute | solution.py:232
  94.5 18.4 %collective-permute-start.8 = (f32[256,512]{1,0:T(8,128)S(1)}, f32[256,512]{1,0:T(8,128)S(1)}, u32[]{:S(2)}, u32[]{:S(2)}) collective-permute-start(f32[256,512]{1,0:T(8,128)S(1)} %get-tuple-element.66), channel_id=1, source_target_pairs={{0,1},{1,0},{2,3},{3,2},{4,5},{5,4},{6,7},{7,6},{8,9},{9,8},{10,11... | collective-permute-start | bytes 1572872 | tf_op jit(solution)/shard_map/ppermute | solution.py:232
  98.3 10.9 %collective-permute-start.4 = (bf16[256,512]{1,0:T(8,128)(2,1)S(1)}, bf16[256,512]{1,0:T(8,128)(2,1)S(1)}, u32[]{:S(2)}, u32[]{:S(2)}) collective-permute-start(bf16[256,512]{1,0:T(8,128)(2,1)S(1)} %collective-permute-done.block_ref), channel_id=1, source_target_pairs={{0,4},{1,13},{2,6},{3,15},{4,8},{5,1},{6,10},{7,3},{8,12},{9,5},{1... | collective-permute-start | bytes 786440 | tf_op jit(solution)/shard_map/ppermute | solution.py:232

commit v3 on v2

--- a/solution.py
+++ b/solution.py
@@ -110,23 +110,20 @@
     add_products(block_ref, rows_ref, slot, refs[:2], refs[2:])
 
 
-def last_kernel(ring, slot, final, me_ref, block_ref, rows_ref, m_ref, t_ref, w_ref, *refs):
-    mine_ref, theirs_ref, ahead_ref, sems = refs
-    rows = [(0, source(me_ref[0], ring, *item)) for item in final]
-    ahead = fetch((w_ref,), rows, ahead_ref, sems)
+def refill_kernel(ring, slot, later, me_ref, block_ref, rows_ref, m_ref, t_ref, *refs):
+    w0_ref, w1_ref, mine_ref, theirs_ref, ahead_ref, sems = refs
+    rows = [(n, source(me_ref[0], ring, *item)) for item in later for n in range(2)]
+    ahead = fetch((w0_ref, w1_ref), rows, ahead_ref, sems)
     add_products(block_ref, rows_ref, slot, (m_ref, t_ref), (mine_ref, theirs_ref))
     for copy in ahead:
         copy.wait()
 
 
-def output_kernel(near_ref, far_ref, w_ref, mine_ref, back_ref, out_ref):
-    rows = mine_ref.shape[0]
-    total = mine_ref[...] + back_ref[...]
-    for n in range(4):
-        pair_ref = (near_ref, far_ref)[n // 2]
-        block = pair_ref[n % 2 * rows : (n % 2 + 1) * rows, :]
-        total = total + jnp.dot(block, w_ref[n], preferred_element_type=jnp.float32)
-    out_ref[...] = total.astype(out_ref.dtype)
+def closing_kernel(slot, block_ref, rows_ref, *refs):
+    total = jnp.dot(block_ref[...], rows_ref[slot], preferred_element_type=jnp.float32)
+    for ref in refs[:-1]:
+        total = total + ref[...]
+    refs[-1][...] = total.astype(refs[-1].dtype)
 
 
 def project(kernel, block, columns, fetched, operands, specs, scratch):
@@ -223,16 +220,12 @@
         2 * rows * width * DH,
     )
 
-    halves = [[2 * y, 2 * y + 1] for y in range(ring)]
     spot = me.reshape(1)
-    order = ((1, True), (1, False), (2, False), (2, True), (3, False))
-    final = ((3, True, 0), (3, True, 1), (4, False, 0), (4, False, 1))
+    early = ((1, True), (1, False), (2, False), (2, True))
+    late = ((4, False), (3, True), (3, False))
 
     def send(block, pairs):
         return lax.ppermute(block, "tp", pairs)
-
-    def share(block):
-        return lax.all_gather(block, "tp", axis=0, tiled=True, axis_index_groups=halves)
 
     def multiply(slot, block, ahead, sums):
         return project(
@@ -248,46 +241,50 @@
     b1 = send(own, across)
     a2 = send(own, onward_two)
     a1 = send(own, onward)
+    b2 = send(b1, onward)
     now = (2, width, out_weight.shape[1])
     *sums, ahead = project(
-        functools.partial(first_kernel, ring, order),
+        functools.partial(first_kernel, ring, early),
         own,
         columns,
-        2 * len(order),
+        2 * len(early),
         (spot, own, *in_hbm(*columns)),
         [SMEM, VMEM, HBM, HBM],
         [pltpu.VMEM(now, out_weight.dtype), pltpu.SemaphoreType.DMA((2,))],
     )
-    b1, sums = tie((b1, sums))
-    b2 = send(b1, onward)
+    a2, sums = tie((a2, sums))
+    a4 = send(a2, onward_two)
+    b3 = send(b2, onward)
+    a3 = send(a2, onward)
     sums = multiply(0, b1, ahead, sums)
     sums = multiply(1, a1, ahead, sums)
-    a2, sums = tie((a2, sums))
-    a4 = send(a2, onward_two)
-    a3 = send(a2, onward)
     sums = multiply(2, a2, ahead, sums)
-    b2, sums = tie((b2, sums))
-    b3 = send(b2, onward)
-    sums = multiply(3, b2, ahead, sums)
-    mine, theirs, rest = project(
-        functools.partial(last_kernel, ring, 8, final),
-        a3,
+    *sums, ahead = project(
+        functools.partial(refill_kernel, ring, 6, late),
+        b2,
         columns,
-        len(final),
-        (spot, a3, ahead, *sums, *in_hbm(out_weight)),
-        [SMEM, VMEM, VMEM, VMEM, VMEM, HBM],
+        2 * len(late),
+        (spot, b2, ahead, *sums, *in_hbm(*columns)),
+        [SMEM, VMEM, VMEM, VMEM, VMEM, HBM, HBM],
         [],
     )
+    a4, sums = tie((a4, sums))
+    sums = multiply(0, a4, ahead, sums)
+    b3, sums = tie((b3, sums))
+    mine, theirs = multiply(1, b3, ahead, sums)
+    a3, theirs = tie((a3, theirs))
+    flops = 2 * rows * width * width
+    shape = (rows, width)
+    theirs = call(
+        functools.partial(closing_kernel, 5), shape, jnp.float32, (a3, ahead, theirs), flops
+    )
     returned = send(theirs, partner)
-    near = share(b3)
-    a4, near = tie((a4, near))
-    far = share(a4)
     return call(
-        output_kernel,
-        (rows, width),
+        functools.partial(closing_kernel, 4),
+        shape,
         jnp.bfloat16,
-        (near, far, rest, mine, returned),
-        8 * rows * width * width,
+        (a3, ahead, mine, returned),
+        flops,
     )
 
 

time: 115 us -> 109 us (0.948)
  blocking collectives: 50.9 us -> 44.9 us
    all_gather x2 -> x0, blocking collectives: 6 us -> none  [share(): lax.all_gather(block, 'tp', axis=0, tiled=True, axis_index_groups=halves)]
    pallas_call x6 -> x7, Pallas kernels: 6.65 us -> 7.28 us  [project(): pl.pallas_call(kernel, out_shape=outs, in_specs=specs, out_specs=[VMEM] *...]
  transfers between devices with their start and end apart: 9 -> 9, of which waited for: 1 -> 3; matrix products, arithmetic and copies ran while one was open for 0% -> 0% of each run, Pallas kernels for 6% -> 7%
where the time goes in v3:
time: 109 us; the launch traced here: 108 us
  starting transfers between devices  47.6 us (44%)
  blocking collectives  44.9 us (41%)
  Pallas kernels  10.9 us (10%)
  waiting for transfers between devices  4.54 us (4%)
    ppermute x8, starting transfers between devices, send(): return lax.ppermute(block, 'tp', pairs)  31.5 us
    all_to_all x1, blocking collectives, on_device(): slices = lax.all_to_all(slices, 'seq', 0, 0, tiled=True)  24 us
    all_to_all x1, blocking collectives, on_device(): prefix = lax.all_to_all(prefix, 'seq', 0, 0, tiled=True).reshape(width, DH)  20.9 us
    ppermute x1, starting transfers between devices, on_device(): columns = (out_weight, lax.ppermute(weight, 'tp', partner))  16 us
    pallas_call x7, Pallas kernels, project(): pl.pallas_call(kernel, out_shape=outs, in_specs=specs, out_specs=[VMEM] *...  7.28 us
    ppermute x8, waiting for transfers between devices, send(): return lax.ppermute(block, 'tp', pairs)  4.53 us
  transfers between devices with their start and end apart: 9, of which 3 were waited for; matrix products, arithmetic and copies ran while one was open for 0% of the time, Pallas kernels for 7%

profile of v3, /device:TPU:1, one launch (start us, length us, event | category | flops | bytes accessed | tf_op | source)
XLA Modules:
  0.0 108.1 jit_solution(6304830971956129522)
XLA Ops:
  0.0 1.9 %shard_map.55 = (bf16[512,128]{1,0:T(8,128)(2,1)S(1)}, f32[256,512]{1,0:T(8,128)S(1)}, bf16[256,512]{1,0:T(8,128)(2,1)S(1)}, f32[1,128]{1,0:T(1,128)S(1)}) custom-call(bf16[256,512]{1,0:T(8,128)(2,1)} %q_hbm.1, bf16[256,512]{1,0:T(8,128)(2,1)} %k_hbm.1, bf16[256,512]{1,0:T(8,128)(2,1)} %v_hbm.1, f32[1,128]{1,0:T(1,128)} %bitcast.6), custom_call_target="tpu_custom_call" | custom-call | flops 167772160 | bytes 786432 | tf_op jit(solution)/shard_map/pallas_call | solution.py:166
  1.9 16.0 %collective-permute-start.1 = (bf16[8192,512]{1,0:T(8,128)(2,1)}, bf16[8192,512]{1,0:T(8,128)(2,1)}, u32[]{:S(2)}, u32[]{:S(2)}) collective-permute-start(bf16[8192,512]{1,0:T(8,128)(2,1)} %refs_0_.1), channel_id=1, source_target_pairs={{0,1},{1,0},{2,3},{3,2},{4,5},{5,4},{6,7},{7,6},{8,9},{9,8},{10,11... | collective-permute-start | bytes 25165832 | tf_op jit(solution)/shard_map/ppermute | solution.py:210
  17.9 24.0 %all_to_all.10.a_ref = bf16[64,8,128]{2,1,0:T(8,128)(2,1)S(1)} all-to-all(bf16[64,8,128]{2,1,0:T(8,128)(2,1)S(1)} %bitcast.5), channel_id=1, replica_groups=mesh['seq'=64,'tp'=16] {'seq'}, dimensions={0} | all-to-all | bytes 262144 | tf_op jit(solution)/shard_map/all_to_all | solution.py:212
  42.0 0.1 shard_map.56
  42.0 20.9 %all_to_all.11 = bf16[64,8,128]{2,1,0:T(8,128)(2,1)S(1)} all-to-all(bf16[64,8,128]{2,1,0:T(8,128)(2,1)S(1)} %shard_map.56), channel_id=1, replica_groups=mesh['seq'=64,'tp'=16] {'seq'}, dimensions={0} | all-to-all | bytes 262144 | tf_op jit(solution)/shard_map/all_to_all | solution.py:214
  62.9 0.4 shard_map.57.block_ref
  63.3 6.2 %collective-permute-start.3 = (bf16[256,512]{1,0:T(8,128)(2,1)S(1)}, bf16[256,512]{1,0:T(8,128)(2,1)S(1)}, u32[]{:S(2)}, u32[]{:S(2)}) collective-permute-start(bf16[256,512]{1,0:T(8,128)(2,1)S(1)} %shard_map.57.block_ref), channel_id=1, source_target_pairs={{1,2},{0,15},{3,4},{2,1},{5,6},{4,3},{7,8},{6,5},{9,10},{8,7},{11,... | collective-permute-start | bytes 786440 | tf_op jit(solution)/shard_map/ppermute | solution.py:228
  69.5 5.0 %collective-permute-start = (bf16[256,512]{1,0:T(8,128)(2,1)S(1)}, bf16[256,512]{1,0:T(8,128)(2,1)S(1)}, u32[]{:S(2)}, u32[]{:S(2)}) collective-permute-start(bf16[256,512]{1,0:T(8,128)(2,1)S(1)} %shard_map.57.block_ref), channel_id=1, source_target_pairs={{0,4},{1,13},{2,6},{3,15},{4,8},{5,1},{6,10},{7,3},{8,12},{9,5},{1... | collective-permute-start | bytes 786440 | tf_op jit(solution)/shard_map/ppermute | solution.py:228
  74.5 0.0 collective-permute-done.3.block_ref
  74.5 3.0 %collective-permute-start.4 = (bf16[256,512]{1,0:T(8,128)(2,1)S(1)}, bf16[256,512]{1,0:T(8,128)(2,1)S(1)}, u32[]{:S(2)}, u32[]{:S(2)}) collective-permute-start(bf16[256,512]{1,0:T(8,128)(2,1)S(1)} %collective-permute-done.3.block_ref), channel_id=1, source_target_pairs={{0,2},{1,15},{2,4},{3,1},{4,6},{5,3},{6,8},{7,5},{8,10},{9,7},{10,... | collective-permute-start | bytes 786440 | tf_op jit(solution)/shard_map/ppermute | solution.py:228
  77.5 3.5 %collective-permute-start.7 = (bf16[256,512]{1,0:T(8,128)(2,1)S(1)}, bf16[256,512]{1,0:T(8,128)(2,1)S(1)}, u32[]{:S(2)}, u32[]{:S(2)}) collective-permute-start(bf16[256,512]{1,0:T(8,128)(2,1)S(1)} %shard_map.57.block_ref), channel_id=1, source_target_pairs={{0,2},{1,15},{2,4},{3,1},{4,6},{5,3},{6,8},{7,5},{8,10},{9,7},{10,... | collective-permute-start | bytes 786440 | tf_op jit(solution)/shard_map/ppermute | solution.py:228
  81.0 0.0 collective-permute-done.1.w1_ref.refs_1_
  81.0 2.9 %shard_map.58 = (f32[256,512]{1,0:T(8,128)S(1)}, f32[256,512]{1,0:T(8,128)S(1)}, bf16[8,512,512]{2,1,0:T(8,128)(2,1)S(1)}) custom-call(s32[1]{0:T(128)} %bitcast.3.me_ref, bf16[256,512]{1,0:T(8,128)(2,1)S(1)} %shard_map.57.block_ref, bf16[8192,512]{1,0:T(8,128)(2,1)} %refs_0_.1, bf16[8192,512]{1,0:T(8,128)(2,1)} %collective-permute-done.1.w1_ref.refs_1_), custom_call_target="tpu_custom_call" | custom-call | flops 268435456 | bytes 5242880 | tf_op jit(solution)/shard_map/pallas_call | solution.py:137
  83.9 0.0 collective-permute-done.block_ref
  83.9 3.8 %collective-permute-start.6 = (bf16[256,512]{1,0:T(8,128)(2,1)S(1)}, bf16[256,512]{1,0:T(8,128)(2,1)S(1)}, u32[]{:S(2)}, u32[]{:S(2)}) collective-permute-start(bf16[256,512]{1,0:T(8,128)(2,1)S(1)} %collective-permute-done.block_ref), channel_id=1, source_target_pairs={{0,4},{1,13},{2,6},{3,15},{4,8},{5,1},{6,10},{7,3},{8,12},{9,5},{1... | collective-permute-start | bytes 786440 | tf_op jit(solution)/shard_map/ppermute | solution.py:228
  87.7 0.0 collective-permute-done.4.block_ref
  87.7 4.0 %collective-permute-start.5 = (bf16[256,512]{1,0:T(8,128)(2,1)S(1)}, bf16[256,512]{1,0:T(8,128)(2,1)S(1)}, u32[]{:S(2)}, u32[]{:S(2)}) collective-permute-start(bf16[256,512]{1,0:T(8,128)(2,1)S(1)} %collective-permute-done.4.block_ref), channel_id=1, source_target_pairs={{0,2},{1,15},{2,4},{3,1},{4,6},{5,3},{6,8},{7,5},{8,10},{9,7},{10,... | collective-permute-start | bytes 786440 | tf_op jit(solution)/shard_map/ppermute | solution.py:228
  91.7 1.9 %collective-permute-start.2 = (bf16[256,512]{1,0:T(8,128)(2,1)S(1)}, bf16[256,512]{1,0:T(8,128)(2,1)S(1)}, u32[]{:S(2)}, u32[]{:S(2)}) collective-permute-start(bf16[256,512]{1,0:T(8,128)(2,1)S(1)} %collective-permute-done.block_ref), channel_id=1, source_target_pairs={{0,2},{1,15},{2,4},{3,1},{4,6},{5,3},{6,8},{7,5},{8,10},{9,7},{10,... | collective-permute-start | bytes 786440 | tf_op jit(solution)/shard_map/ppermute | solution.py:228
  93.7 0.4 shard_map.59
  94.1 0.0 collective-permute-done.7.block_ref
  94.1 0.4 shard_map.60
  94.6 0.4 shard_map.61
  95.0 2.2 %shard_map.62 = (f32[256,512]{1,0:T(8,128)S(1)}, f32[256,512]{1,0:T(8,128)S(1)}, bf16[6,512,512]{2,1,0:T(8,128)(2,1)S(1)}) custom-call(s32[1]{0:T(128)} %bitcast.3.me_ref, bf16[256,512]{1,0:T(8,128)(2,1)S(1)} %collective-permute-done.4.block_ref, bf16[8,512,512]{2,1,0:T(8,128)(2,1)S(1)} %get-tuple-element.47.rows_ref, ...), custom_call_target="tpu_custom_call" | custom-call | flops 268435456 | bytes 4194304 | tf_op jit(solution)/shard_map/pallas_call | solution.py:137
  97.2 0.0 collective-permute-done.6.block_ref
  97.3 0.4 shard_map.63
  97.7 0.6 collective-permute-done.5.block_ref
  98.3 0.4 shard_map.64
  98.8 2.4 %collective-permute-done.2.block_ref = bf16[256,512]{1,0:T(8,128)(2,1)S(1)} collective-permute-done((bf16[256,512]{1,0:T(8,128)(2,1)S(1)}, bf16[256,512]{1,0:T(8,128)(2,1)S(1)}, u32[]{:S(2)}, u32[]{:S(2)}) %collective-permute-start.2) | collective-permute-done | bytes 262176 | tf_op jit(solution)/shard_map/ppermute | solution.py:228
  101.2 0.3 shard_map.65
  101.5 4.1 %collective-permute-start.8 = (f32[256,512]{1,0:T(8,128)S(1)}, f32[256,512]{1,0:T(8,128)S(1)}, u32[]{:S(2)}, u32[]{:S(2)}) collective-permute-start(f32[256,512]{1,0:T(8,128)S(1)} %shard_map.65), channel_id=1, source_target_pairs={{0,1},{1,0},{2,3},{3,2},{4,5},{5,4},{6,7},{7,6},{8,9},{9,8},{10,11... | collective-permute-start | bytes 1572872 | tf_op jit(solution)/shard_map/ppermute | solution.py:228
  105.6 1.5 %collective-permute-done.8.refs_1_ = f32[256,512]{1,0:T(8,128)S(1)} collective-permute-done((f32[256,512]{1,0:T(8,128)S(1)}, f32[256,512]{1,0:T(8,128)S(1)}, u32[]{:S(2)}, u32[]{:S(2)}) %collective-permute-start.8) | collective-permute-done | bytes 524320 | tf_op jit(solution)/shard_map/ppermute | solution.py:228
  107.1 1.0 shard_map.66
Async XLA Ops:
  1.9 79.1 %collective-permute-start.1 = (bf16[8192,512]{1,0:T(8,128)(2,1)}, bf16[8192,512]{1,0:T(8,128)(2,1)}, u32[]{:S(2)}, u32[]{:S(2)}) collective-permute-start(bf16[8192,512]{1,0:T(8,128)(2,1)} %refs_0_.1), channel_id=1, source_target_pairs={{0,1},{1,0},{2,3},{3,2},{4,5},{5,4},{6,7},{7,6},{8,9},{9,8},{10,11... | collective-permute-start | bytes 25165832 | tf_op jit(solution)/shard_map/ppermute | solution.py:210
  63.3 11.2 %collective-permute-start.3 = (bf16[256,512]{1,0:T(8,128)(2,1)S(1)}, bf16[256,512]{1,0:T(8,128)(2,1)S(1)}, u32[]{:S(2)}, u32[]{:S(2)}) collective-permute-start(bf16[256,512]{1,0:T(8,128)(2,1)S(1)} %shard_map.57.block_ref), channel_id=1, source_target_pairs={{1,2},{0,15},{3,4},{2,1},{5,6},{4,3},{7,8},{6,5},{9,10},{8,7},{11,... | collective-permute-start | bytes 786440 | tf_op jit(solution)/shard_map/ppermute | solution.py:228
  69.5 14.4 %collective-permute-start = (bf16[256,512]{1,0:T(8,128)(2,1)S(1)}, bf16[256,512]{1,0:T(8,128)(2,1)S(1)}, u32[]{:S(2)}, u32[]{:S(2)}) collective-permute-start(bf16[256,512]{1,0:T(8,128)(2,1)S(1)} %shard_map.57.block_ref), channel_id=1, source_target_pairs={{0,4},{1,13},{2,6},{3,15},{4,8},{5,1},{6,10},{7,3},{8,12},{9,5},{1... | collective-permute-start | bytes 786440 | tf_op jit(solution)/shard_map/ppermute | solution.py:228
  74.5 13.2 %collective-permute-start.4 = (bf16[256,512]{1,0:T(8,128)(2,1)S(1)}, bf16[256,512]{1,0:T(8,128)(2,1)S(1)}, u32[]{:S(2)}, u32[]{:S(2)}) collective-permute-start(bf16[256,512]{1,0:T(8,128)(2,1)S(1)} %collective-permute-done.3.block_ref), channel_id=1, source_target_pairs={{0,2},{1,15},{2,4},{3,1},{4,6},{5,3},{6,8},{7,5},{8,10},{9,7},{10,... | collective-permute-start | bytes 786440 | tf_op jit(solution)/shard_map/ppermute | solution.py:228
  77.5 16.6 %collective-permute-start.7 = (bf16[256,512]{1,0:T(8,128)(2,1)S(1)}, bf16[256,512]{1,0:T(8,128)(2,1)S(1)}, u32[]{:S(2)}, u32[]{:S(2)}) collective-permute-start(bf16[256,512]{1,0:T(8,128)(2,1)S(1)} %shard_map.57.block_ref), channel_id=1, source_target_pairs={{0,2},{1,15},{2,4},{3,1},{4,6},{5,3},{6,8},{7,5},{8,10},{9,7},{10,... | collective-permute-start | bytes 786440 | tf_op jit(solution)/shard_map/ppermute | solution.py:228
  83.9 13.3 %collective-permute-start.6 = (bf16[256,512]{1,0:T(8,128)(2,1)S(1)}, bf16[256,512]{1,0:T(8,128)(2,1)S(1)}, u32[]{:S(2)}, u32[]{:S(2)}) collective-permute-start(bf16[256,512]{1,0:T(8,128)(2,1)S(1)} %collective-permute-done.block_ref), channel_id=1, source_target_pairs={{0,4},{1,13},{2,6},{3,15},{4,8},{5,1},{6,10},{7,3},{8,12},{9,5},{1... | collective-permute-start | bytes 786440 | tf_op jit(solution)/shard_map/ppermute | solution.py:228
  87.7 10.7 %collective-permute-start.5 = (bf16[256,512]{1,0:T(8,128)(2,1)S(1)}, bf16[256,512]{1,0:T(8,128)(2,1)S(1)}, u32[]{:S(2)}, u32[]{:S(2)}) collective-permute-start(bf16[256,512]{1,0:T(8,128)(2,1)S(1)} %collective-permute-done.4.block_ref), channel_id=1, source_target_pairs={{0,2},{1,15},{2,4},{3,1},{4,6},{5,3},{6,8},{7,5},{8,10},{9,7},{10,... | collective-permute-start | bytes 786440 | tf_op jit(solution)/shard_map/ppermute | solution.py:228
  91.7 9.4 %collective-permute-start.2 = (bf16[256,512]{1,0:T(8,128)(2,1)S(1)}, bf16[256,512]{1,0:T(8,128)(2,1)S(1)}, u32[]{:S(2)}, u32[]{:S(2)}) collective-permute-start(bf16[256,512]{1,0:T(8,128)(2,1)S(1)} %collective-permute-done.block_ref), channel_id=1, source_target_pairs={{0,2},{1,15},{2,4},{3,1},{4,6},{5,3},{6,8},{7,5},{8,10},{9,7},{10,... | collective-permute-start | bytes 786440 | tf_op jit(solution)/shard_map/ppermute | solution.py:228
  101.5 5.7 %collective-permute-start.8 = (f32[256,512]{1,0:T(8,128)S(1)}, f32[256,512]{1,0:T(8,128)S(1)}, u32[]{:S(2)}, u32[]{:S(2)}) collective-permute-start(f32[256,512]{1,0:T(8,128)S(1)} %shard_map.65), channel_id=1, source_target_pairs={{0,1},{1,0},{2,3},{3,2},{4,5},{5,4},{6,7},{7,6},{8,9},{9,8},{10,11... | collective-permute-start | bytes 1572872 | tf_op jit(solution)/shard_map/ppermute | solution.py:228
